TPU v7x, 32 devices: a whole 2x2x4 slice. The times are simulated.
32 devices in a mesh: dp: 8 (over y, x, core), tensor: 4 (over z).
Axes of the slice: x: 2, y: 2, z: 4, core: 2. Of those that a mesh axis runs over, the one named last changes fastest.
Arguments:
- hidden_in: bfloat16 [16384, 1024], P('dp'), may hold values from -6 to 6
- lengths: int32 [8], P('dp'), may hold values from 512 to 2048, as said below
- query_weight: bfloat16 [1024, 1024], P(None, 'tensor'), may hold values from -0.1875 to 0.1875
- query_bias: bfloat16 [1024], P('tensor'), may hold values from -1 to 1
- key_weight: bfloat16 [1024, 1024], P(None, 'tensor'), may hold values from -0.1875 to 0.1875
- value_weight: bfloat16 [1024, 1024], P(None, 'tensor'), may hold values from -0.1875 to 0.1875
- value_bias: bfloat16 [1024], P('tensor'), may hold values from -1 to 1
- output_weight: bfloat16 [1024, 1024], P(None, 'tensor'), may hold values from -2 to 2
- output_bias: bfloat16 [1024], replicated, may hold values from -1 to 1
- first_gain: bfloat16 [1024], replicated, may hold values from 0.5 to 1.5
- first_shift: bfloat16 [1024], replicated, may hold values from -1 to 1
- inner_weight: bfloat16 [1024, 4096], P(None, 'tensor'), may hold values from -0.1875 to 0.1875
- inner_bias: bfloat16 [4096], P('tensor'), may hold values from -1 to 1
- outer_weight: bfloat16 [1024, 4096], P(None, 'tensor'), may hold values from -0.125 to 0.125
- outer_bias: bfloat16 [1024], replicated, may hold values from -1 to 1
- second_gain: bfloat16 [1024], replicated, may hold values from 0.5 to 1.5
- second_shift: bfloat16 [1024], replicated, may hold values from -1 to 1
- cotangent: bfloat16 [16384, 1024], P('dp'), may hold values from -6 to 6
- teacher: bfloat16 [16384, 1024], P('dp'), may hold values from -6 to 6
Outputs:
- layer_output: bfloat16 [16384, 1024], P(('dp', 'tensor'))
- distill_loss: float32 [], replicated
- input_grad: float32 [16384, 1024], P(('dp', 'tensor'))
- query_weight_grad: float32 [1024, 1024], P('dp', 'tensor')
- query_bias_grad: float32 [1024], replicated
- key_weight_grad: float32 [1024, 1024], P('dp', 'tensor')
- value_weight_grad: float32 [1024, 1024], P('dp', 'tensor')
- value_bias_grad: float32 [1024], replicated
- output_weight_grad: float32 [1024, 1024], P('dp', 'tensor')
- output_bias_grad: float32 [1024], replicated
- first_gain_grad: float32 [1024], replicated
- first_shift_grad: float32 [1024], replicated
- inner_weight_grad: float32 [1024, 4096], P('dp', 'tensor')
- inner_bias_grad: float32 [4096], replicated
- outer_weight_grad: float32 [1024, 4096], P('dp', 'tensor')
- outer_bias_grad: float32 [1024], replicated
- second_gain_grad: float32 [1024], replicated
- second_shift_grad: float32 [1024], replicated
Inputs may be any that keep to these rules, and one draw needn't show every extreme that they name: `lengths`: one sequence's valid tokens; slots after them are padding; some sequence fills all 2048 slots.
All inputs are finite; a program needn't handle non-finite values.
Results may differ from a plain program's by a relative error of at most 0.018.
Values may be sent and summed in bfloat16 or wider, within the bound.
No kernel may reach another device: no remote copies, remote signals or barrier semaphores. Data moves between devices by JAX's collectives and lax.ppermute only.
A program may use at most 256 MiB of HBM per device.

v0:
```python
import jax
import jax.numpy as jnp
from jax import lax
from jax.experimental import pallas as pl
from jax.experimental.pallas import tpu as pltpu
from jax.sharding import PartitionSpec as P

HD = 64
PAIR = 128
VMEM_BYTES = 60000 * 1024


epsilon = 1e-05


def matmul(former, latter):
    return jnp.dot(former, latter, preferred_element_type=jnp.float32)


def times_rows(former, latter):
    return lax.dot_general(
        former, latter, (((1,), (1,)), ((), ())), preferred_element_type=jnp.float32
    )


def over_rows(former, latter):
    return lax.dot_general(
        former, latter, (((0,), (0,)), ((), ())), preferred_element_type=jnp.float32
    )


def layer_norm(hidden, norm_gain, norm_shift):
    centered = hidden - jnp.mean(hidden, axis=-1, keepdims=True)
    inverse = lax.rsqrt(jnp.mean(centered * centered, axis=-1, keepdims=True) + epsilon)
    normal = centered * inverse
    return (normal * norm_gain + norm_shift, normal, inverse)


def norm_back(upstream, normal, inverse, norm_gain):
    scaled = upstream * norm_gain
    return inverse * (
        scaled
        - jnp.mean(scaled, axis=-1, keepdims=True)
        - normal * jnp.mean(scaled * normal, axis=-1, keepdims=True)
    )


def gelu_parts(values):
    cumulative = 0.5 * (1.0 + jax.scipy.special.erf(values * 0.7071067811865476))
    slope = cumulative + values * jnp.exp(-0.5 * values * values) * 0.3989422804014327
    return (values * cumulative, slope)


def lanes(rows):
    return lax.broadcasted_iota(jnp.int32, (rows, PAIR), 1)


def in_head(lane, head):
    return (lane < HD) if head == 0 else (lane >= HD)


def extend(base, lane, head, first, offset):
    start = HD * (1 - head)
    high = offset.astype(jnp.bfloat16).astype(jnp.float32)
    middle = (offset - high).astype(jnp.bfloat16).astype(jnp.float32)
    out = jnp.where(lane == start, first, 0.0)
    out = jnp.where(lane == start + 1, -high, out)
    out = jnp.where(lane == start + 2, -middle, out)
    out = jnp.where(lane == start + 3, high + middle - offset, out)
    return jnp.where(in_head(lane, head), base, out).astype(jnp.bfloat16)


def extend_keys(keys, lane, head, row_start, length):
    start = HD * (1 - head)
    position = row_start + lax.broadcasted_iota(jnp.int32, keys.shape, 0)
    bias = jnp.where(position < length, 0.0, -1e30)
    ones = jnp.where((lane > start) & (lane < start + 4), 1.0, 0.0)
    side = jnp.where(lane == start, bias, ones)
    return jnp.where(in_head(lane, head), keys, side).astype(jnp.bfloat16)


def extend_values(values, lane, head):
    return jnp.where(in_head(lane, head), values, 1.0).astype(jnp.bfloat16)


def forward_kernel(length_ref, q_ref, k_ref, v_ref, context_ref, extended_ref, keys, values):
    @pl.when(pl.program_id(1) == 0)
    def _():
        lane = lanes(k_ref.shape[0])
        k_float = k_ref[...].astype(jnp.float32)
        v_float = v_ref[...].astype(jnp.float32)
        for head in range(2):
            keys[head] = extend_keys(k_float, lane, head, 0, length_ref[0])
            values[head] = extend_values(v_float, lane, head)

    lane = lanes(q_ref.shape[0])
    scaled = q_ref[...].astype(jnp.float32) * HD**-0.5
    contexts = []
    for head in range(2):
        plain = jnp.where(lane == HD * (1 - head), 1.0, 0.0)
        query = jnp.where(in_head(lane, head), scaled, plain).astype(jnp.bfloat16)
        scores = times_rows(query, keys[head])
        peak = jnp.max(scores, axis=1, keepdims=True)
        exponent = jnp.exp(scores - peak).astype(jnp.bfloat16)
        out = matmul(exponent, values[head])
        contexts.append(out / pltpu.roll(out, HD, 1))
        extended_ref[head] = extend(scaled, lane, head, 1.0, peak + jnp.log(out))
    context_ref[...] = jnp.where(lane < HD, contexts[0], contexts[1]).astype(jnp.bfloat16)


def attend_forward(length, qkv):
    seq_len = qkv.shape[0]
    pairs = qkv.shape[1] // (3 * PAIR)
    rows = min(256, seq_len)
    return pl.pallas_call(
        forward_kernel,
        grid_spec=pltpu.PrefetchScalarGridSpec(
            num_scalar_prefetch=1,
            grid=(pairs, seq_len // rows),
            in_specs=[
                pl.BlockSpec((rows, PAIR), lambda p, i, n: (i, 3 * p)),
                pl.BlockSpec((seq_len, PAIR), lambda p, i, n: (0, 3 * p + 1)),
                pl.BlockSpec((seq_len, PAIR), lambda p, i, n: (0, 3 * p + 2)),
            ],
            out_specs=[
                pl.BlockSpec((rows, PAIR), lambda p, i, n: (i, p)),
                pl.BlockSpec((2, rows, PAIR), lambda p, i, n: (p, i, 0)),
            ],
            scratch_shapes=[pltpu.VMEM((2, seq_len, PAIR), jnp.bfloat16)] * 2,
        ),
        out_shape=[
            jax.ShapeDtypeStruct((seq_len, pairs * PAIR), jnp.bfloat16),
            jax.ShapeDtypeStruct((2 * pairs, seq_len, PAIR), jnp.bfloat16),
        ],
        compiler_params=pltpu.CompilerParams(vmem_limit_bytes=VMEM_BYTES),
        cost_estimate=pl.CostEstimate(
            flops=8 * seq_len * seq_len * 2 * PAIR * pairs,
            bytes_accessed=12 * seq_len * PAIR * pairs,
            transcendentals=2 * seq_len * seq_len * pairs,
        ),
        name="attend_forward",
    )(length, qkv, qkv, qkv)


def backward_kernel(length_ref, extended_ref, k_ref, v_ref, context_ref, grad_ref, out_ref, grads, turned):
    step = pl.program_id(0)
    seq_len, rows = grad_ref.shape[0], k_ref.shape[0]

    @pl.when(step == 0)
    def _():
        def prepare(j, carry):
            here = pl.ds(pl.multiple_of(j * rows, rows), rows)
            lane = lanes(rows)
            grad = grad_ref[here, :].astype(jnp.float32)
            product = grad * context_ref[here, :].astype(jnp.float32)
            for head in range(2):
                centre = jnp.sum(
                    jnp.where(in_head(lane, head), product, 0.0), axis=1, keepdims=True
                )
                grads[head, here, :] = extend(grad, lane, head, 0.0, centre)
            return carry

        lax.fori_loop(0, seq_len // rows, prepare, 0)

    lane = lanes(rows)
    k_float = k_ref[...].astype(jnp.float32)
    v_float = v_ref[...].astype(jnp.float32)
    across = k_float.T.astype(jnp.bfloat16)
    key_grads, value_grads = [], []
    for head in range(2):
        keys = extend_keys(k_float, lane, head, step * rows, length_ref[0])
        values = extend_values(v_float, lane, head)
        query, grad = extended_ref[head], grads[head]
        probs = jnp.exp(times_rows(keys, query))
        score_grad = (probs * times_rows(values, grad)).astype(jnp.bfloat16)
        value_grads.append(matmul(probs.astype(jnp.bfloat16), grad))
        key_grads.append(matmul(score_grad, query))
        own = slice(HD * head, HD * (head + 1))
        part = matmul(across[own], score_grad)

        @pl.when(step == 0)
        def _():
            turned[own, :] = part

        @pl.when(step > 0)
        def _():
            turned[own, :] += part

    here = pl.ds(pl.multiple_of(step * rows, rows), rows)
    key_grad = jnp.where(lane < HD, key_grads[0], key_grads[1])
    value_grad = jnp.where(lane < HD, value_grads[0], value_grads[1])
    out_ref[here, PAIR : 2 * PAIR] = key_grad.astype(jnp.bfloat16)
    out_ref[here, 2 * PAIR :] = value_grad.astype(jnp.bfloat16)

    @pl.when(step == pl.num_programs(0) - 1)
    def _():
        def finish(j, carry):
            here = pl.ds(pl.multiple_of(j * rows, rows), rows)
            out_ref[here, :PAIR] = (turned[:, here].T * HD**-0.5).astype(jnp.bfloat16)
            return carry

        lax.fori_loop(0, seq_len // rows, finish, 0)


def attend_backward(length, extended, qkv, context, context_grad, pair):
    seq_len = qkv.shape[0]
    rows = min(256, seq_len)
    return pl.pallas_call(
        backward_kernel,
        grid_spec=pltpu.PrefetchScalarGridSpec(
            num_scalar_prefetch=1,
            grid=(seq_len // rows,),
            in_specs=[
                pl.BlockSpec((2, seq_len, PAIR), lambda i, n: (pair, 0, 0)),
                pl.BlockSpec((rows, PAIR), lambda i, n: (i, 3 * pair + 1)),
                pl.BlockSpec((rows, PAIR), lambda i, n: (i, 3 * pair + 2)),
                pl.BlockSpec((seq_len, PAIR), lambda i, n: (0, pair)),
                pl.BlockSpec((seq_len, PAIR), lambda i, n: (0, pair)),
            ],
            out_specs=pl.BlockSpec((seq_len, 3 * PAIR), lambda i, n: (0, 0)),
            scratch_shapes=[
                pltpu.VMEM((2, seq_len, PAIR), jnp.bfloat16),
                pltpu.VMEM((PAIR, seq_len), jnp.float32),
            ],
        ),
        out_shape=jax.ShapeDtypeStruct((seq_len, 3 * PAIR), jnp.bfloat16),
        compiler_params=pltpu.CompilerParams(vmem_limit_bytes=VMEM_BYTES),
        cost_estimate=pl.CostEstimate(
            flops=20 * seq_len * seq_len * 2 * PAIR,
            bytes_accessed=20 * seq_len * PAIR,
            transcendentals=2 * seq_len * seq_len,
        ),
        name="attend_backward",
    )(length, extended, qkv, qkv, context, context_grad)


def tie(*values):
    return lax.optimization_barrier(values)


def flip(array_in, axis_name, bits):
    size = lax.axis_size(axis_name)
    return lax.ppermute(array_in, axis_name, [(i, i ^ bits) for i in range(size)])


def total(array_in, axis_names):
    for name in axis_names:
        bits = 1
        while bits < lax.axis_size(name):
            array_in = array_in + flip(array_in, name, bits)
            bits *= 2
    return array_in


def shards(
    hidden_in,
    lengths,
    query_weight,
    query_bias,
    key_weight,
    value_weight,
    value_bias,
    output_weight,
    output_bias,
    first_gain,
    first_shift,
    inner_weight,
    inner_bias,
    outer_weight,
    outer_bias,
    second_gain,
    second_shift,
    cotangent,
    teacher,
):
    seq_len, model_width = hidden_in.shape
    ranks = lax.axis_size("tensor")
    rank = lax.axis_index("tensor")
    copies = lax.axis_size("dp")
    copy = lax.axis_index("dp")
    share_rows = seq_len // ranks
    heads_width = query_weight.shape[1]
    units = inner_weight.shape[1]
    pairs = heads_width // PAIR
    row_valid = jnp.arange(seq_len, dtype=jnp.int32) < lengths[0]

    def take_own(array_in):
        return lax.dynamic_slice_in_dim(array_in, rank * share_rows, share_rows, 0)

    def by_pairs(*arrays):
        return jnp.concatenate(
            [a[..., p * PAIR : (p + 1) * PAIR] for p in range(pairs) for a in arrays], axis=-1
        )

    def own_part(weight):
        rows = weight.shape[0] // copies
        return lax.dynamic_slice_in_dim(weight, copy * rows, rows, 0)

    def others(part):
        return jnp.stack([flip(part, "tensor", s) for s in range(1, ranks)])

    def gathered(parts):
        return lax.all_gather(parts, "dp", axis=1, tiled=True)

    def trade(blocks):
        return lax.all_to_all(blocks, "tensor", 0, 0)

    def block_of(blocks, s):
        return lax.dynamic_index_in_dim(blocks, rank ^ s, 0, keepdims=False)

    def reordered(blocks):
        return jnp.stack([block_of(blocks, s) for s in range(ranks)])

    def column_blocks(array_in):
        width = array_in.shape[1] // ranks
        return jnp.stack(
            [
                lax.dynamic_slice_in_dim(array_in, (rank ^ i) * width, width, 1)
                for i in range(ranks)
            ]
        )

    def add_blocks(blocks):
        return sum(blocks[i].astype(jnp.float32) for i in range(ranks))

    def ordered(vector_in):
        table = vector_in.reshape(ranks, -1)
        return jnp.concatenate(
            [lax.dynamic_index_in_dim(table, rank ^ s, 0, keepdims=False) for s in range(ranks)]
        )

    def half_columns(array_in, other):
        blocks = jnp.split(array_in, copies, axis=1)
        odd = ((copy & 1) ^ other) == 1
        return jnp.concatenate(
            [jnp.where(odd, blocks[i + 1], blocks[i]) for i in range(0, copies, 2)], axis=1
        )

    def half_rows(whole, other):
        blocks = whole.reshape(copies // 2, 2, -1, whole.shape[1])
        mine = lax.dynamic_index_in_dim(blocks, (copy & 1) ^ other, 1, keepdims=False)
        return mine.reshape(-1, whole.shape[1])

    def with_other_core(kept, given):
        come = flip(given, "dp", 1).astype(jnp.float32)
        return (kept.astype(jnp.float32) + come).astype(jnp.bfloat16)

    def qkv_product(qkv_low):
        return [matmul(half, qkv_low).astype(jnp.bfloat16) for half in hidden_halves]

    def halves_of(kept):
        places = list(range(1, copies.bit_length() - 1))
        states = []
        for part, order in zip(jnp.split(kept, 2, axis=1), (places[::-1], places)):
            states.append((part.reshape(copies // 2, -1, part.shape[1]), list(places), order))
        return states

    def begin(states):
        started = []
        for blocks, left, order in states:
            place = order[0]
            low = 2 ** sum(p < place for p in left)
            split = blocks.reshape(-1, 2, low, *blocks.shape[1:])
            mine = (copy >> place) & 1
            keep = lax.dynamic_index_in_dim(split, mine, 1, keepdims=False)
            give = lax.dynamic_index_in_dim(split, 1 - mine, 1, keepdims=False)
            started.append((keep, flip(give, "dp", 1 << place)))
        return started

    def complete(states, started):
        out = []
        for (blocks, left, order), (keep, come) in zip(states, started):
            added = keep.astype(jnp.float32) + come.astype(jnp.float32)
            added = added.astype(jnp.bfloat16).reshape(-1, *blocks.shape[1:])
            out.append((added, [p for p in left if p != order[0]], order[1:]))
        return out

    def step(states):
        return complete(states, begin(states))

    def finished(states):
        while states[0][2]:
            states = step(states)
        return jnp.concatenate([blocks[0] for blocks, _, _ in states], axis=1)

    def scatter_copies(whole):
        return lax.psum_scatter(whole, "dp", scatter_dimension=0, tiled=True)

    def column_sums(array_in):
        return jnp.sum(array_in.astype(jnp.float32), axis=0)

    qkv_weight = by_pairs(query_weight, key_weight, value_weight)
    qkv_bias = by_pairs(query_bias, jnp.zeros_like(query_bias), value_bias)
    output_part, both_part = own_part(output_weight), own_part(
        jnp.concatenate([inner_weight, outer_weight], axis=1)
    )
    part_rows = output_part.shape[0]
    bias_rows = inner_bias.reshape(-1, heads_width)
    output_part = jnp.concatenate([output_part, bias_rows, jnp.zeros_like(bias_rows)])
    output_parts = trade(jnp.broadcast_to(output_part, (ranks, *output_part.shape)))
    near_part = flip(both_part, "tensor", 1)
    qkv_part = own_part(qkv_weight)
    qkv = (matmul(hidden_in, qkv_weight) + qkv_bias).astype(jnp.bfloat16)
    output_parts, near_part, qkv = tie(output_parts, near_part, qkv)
    far_parts = [flip(both_part, "tensor", s) for s in range(2, ranks)]
    output_others = [block_of(output_parts, s) for s in range(1, ranks)]
    output_rest = [p[:part_rows] for p in output_others]
    biases = [p[part_rows : part_rows + bias_rows.shape[0]] for p in output_others]

    column = lax.broadcasted_iota(jnp.int32, (part_rows, PAIR), 1)
    digits = jnp.where(column == 0, lengths[0] // 256, lengths[0] % 256).astype(jnp.bfloat16)
    near_rows = lax.all_gather(
        jnp.concatenate([near_part, *output_rest, digits], axis=1), "dp", axis=0, tiled=True
    )
    context, extended = attend_forward(lengths, qkv)
    received = trade(context.reshape(ranks, share_rows, heads_width))
    far_parts, context, hidden_late = tie(far_parts, context, hidden_in)
    far_rows = gathered(jnp.stack(far_parts))
    hidden_halves = [half_columns(hidden_late, other).T for other in range(2)]
    received, hidden_halves = tie(received, hidden_halves)
    digits = near_rows[::part_rows, -PAIR:].astype(jnp.float32)
    token_total = jnp.sum(256.0 * digits[:, 0] + digits[:, 1])
    grad_scale = seq_len * copies / (2.0 * token_total)
    context_all = jnp.concatenate(
        [block_of(received, s) for s in range(ranks)], axis=1
    )
    both_rest = [near_rows[:, : 2 * units]] + [far_rows[i] for i in range(ranks - 2)]
    inner_weights = [inner_weight] + [rest[:, :units] for rest in both_rest]
    outer_weights = [outer_weight] + [rest[:, units:] for rest in both_rest]
    inner_biases = [inner_bias] + [b.reshape(-1) for b in biases]
    output_weight_all = jnp.concatenate([output_weight, near_rows[:, 2 * units : -PAIR]], axis=1)

    hidden_own = take_own(hidden_in).astype(jnp.float32)
    attention = times_rows(context_all, output_weight_all)
    normed, normal_one, inverse_one = layer_norm(
        hidden_own + (attention + output_bias), first_gain, first_shift
    )
    normed_low = normed.astype(jnp.bfloat16)
    activated, slopes = [], []
    branch = outer_bias.astype(jnp.float32)
    for s in range(ranks):
        value, slope = gelu_parts(matmul(normed_low, inner_weights[s]) + inner_biases[s])
        activated.append(value.astype(jnp.bfloat16))
        slopes.append(slope.astype(jnp.bfloat16))
        branch = branch + times_rows(activated[s], outer_weights[s])
    final, normal_two, inverse_two = layer_norm(normed + branch, second_gain, second_shift)
    row_mask = take_own(row_valid)[:, None]
    difference = final - take_own(teacher).astype(jnp.float32)
    loss_part = jnp.sum(jnp.where(row_mask, difference * difference, 0.0))
    final_grad = jnp.where(
        row_mask, take_own(cotangent).astype(jnp.float32) + grad_scale * difference, 0.0
    )
    second_grad = norm_back(final_grad, normal_two, inverse_two, second_gain)
    branch_low = second_grad.astype(jnp.bfloat16)
    outer_whole = over_rows(branch_low, jnp.concatenate(activated, axis=1)).astype(jnp.bfloat16)
    outer_whole, branch_low, qkv_part = tie(outer_whole, branch_low, qkv_part)
    outer_rows = scatter_copies(outer_whole)
    qkv_parts = others(qkv_part)
    inner_lows = []
    normed_grad = second_grad
    for s in range(ranks):
        inner_low = (matmul(branch_low, outer_weights[s]) * slopes[s]).astype(jnp.bfloat16)
        inner_lows.append(inner_low)
        normed_grad = normed_grad + times_rows(inner_low, inner_weights[s])
    first_grad = norm_back(normed_grad, normal_one, inverse_one, first_gain)
    attention_low = first_grad.astype(jnp.bfloat16)
    grad_all = matmul(attention_low, output_weight_all).astype(jnp.bfloat16)
    grad_all, inner_lows, qkv_parts = tie(grad_all, inner_lows, qkv_parts)
    qkv_rest = gathered(qkv_parts)
    context_grad = trade(column_blocks(grad_all)).reshape(seq_len, heads_width)
    inner_whole = over_rows(normed_low, jnp.concatenate(inner_lows, axis=1)).astype(jnp.bfloat16)
    inner_kept = with_other_core(half_rows(inner_whole, 0), half_rows(inner_whole, 1))
    output_whole = over_rows(attention_low, context_all).astype(jnp.bfloat16)
    inner_states = halves_of(inner_kept)
    inner_started = begin(inner_states)
    vectors = [
        ordered(jnp.concatenate([column_sums(low) for low in inner_lows])),
        column_sums(attention_low),
        column_sums(normed_grad * normal_one),
        column_sums(normed_grad),
        column_sums(branch_low),
        column_sums(final_grad * normal_two),
        column_sums(final_grad),
        ordered(column_sums(grad_all)),
        jnp.full((model_width,), loss_part),
    ]
    vectors = jnp.concatenate([v.reshape(-1, model_width) for v in vectors])
    vectors = vectors + flip(vectors, "dp", 1)
    context_grad, inner_kept, vectors, output_whole = tie(
        context_grad, inner_kept, vectors, output_whole
    )
    output_rows = scatter_copies(output_whole)
    outer_come = trade(column_blocks(outer_rows))
    rank_bits = [1 << p for p in range(ranks.bit_length() - 1)]
    vector_come = flip(vectors, "tensor", rank_bits[0])

    def add_input(rows, moved, pair):
        columns = slice(3 * PAIR * pair, 3 * PAIR * (pair + 1))
        blocks = jnp.concatenate([block_of(moved, s) for s in range(ranks)], axis=1)
        weights = [qkv_weight] + [qkv_rest[s] for s in range(ranks - 1)]
        return rows + times_rows(blocks, jnp.concatenate([w[:, columns] for w in weights], axis=1))

    input_rows = first_grad
    query_sums = []
    for pair in range(pairs):
        qkv_low = attend_backward(lengths, extended, qkv, context, context_grad, pair)
        if pair == 0:
            qkv_low, inner_started, outer_come, vector_come = tie(
                qkv_low, inner_started, outer_come, vector_come
            )
            outer_weight_grad = add_blocks(outer_come)
            inner_states = complete(inner_states, inner_started)
            inner_started = begin(inner_states) if inner_states[0][2] else None
            vectors = vectors + vector_come
            vector_come = flip(vectors, "tensor", rank_bits[1])
        if pair == 0:
            qkv_kept = [with_other_core(*qkv_product(qkv_low))]
            context_grad, qkv_kept = tie(context_grad, qkv_kept)
        else:
            moved, qkv_low, inner_started, vector_come, output_rows, qkv_rest = tie(
                moved, qkv_low, inner_started, vector_come, output_rows, qkv_rest
            )
            vectors = vectors + vector_come
            input_rows = add_input(input_rows, moved, pair - 1)
            qkv_kept.append(with_other_core(*qkv_product(qkv_low)))
        moved = trade(qkv_low.reshape(ranks, share_rows, -1))
        query_sums.append(column_sums(qkv_low[:, :PAIR]))
    inner_states = complete(inner_states, inner_started)
    inner_parts = finished(inner_states)
    if pairs == 1:
        vectors = vectors + vector_come
    for bit in rank_bits[2:]:
        vectors = vectors + flip(vectors, "tensor", bit)
    query_sums = jnp.concatenate(query_sums)
    query_sums = query_sums + flip(query_sums, "dp", 1)
    query_row = jnp.pad(query_sums, (0, model_width - heads_width))[None]
    vectors = jnp.concatenate([vectors, query_row])
    for place in range(1, copies.bit_length() - 1):
        vectors = vectors + flip(vectors, "dp", 1 << place)
    query_sums = vectors[-1, :heads_width]

    high = query_sums.astype(jnp.bfloat16)
    middle = (query_sums - high.astype(jnp.float32)).astype(jnp.bfloat16)
    low = query_sums - high.astype(jnp.float32) - middle.astype(jnp.float32)
    digit_rows = jnp.stack([high, middle, low.astype(jnp.bfloat16)])
    digit_rows = jnp.pad(digit_rows, ((0, 5), (units, 0)))
    rows = [inner_parts, output_rows]
    rows = [[jnp.split(r, ranks, axis=1)[s] for r in rows] for s in range(ranks)]
    last = [jnp.concatenate([jnp.concatenate(r, axis=1), digit_rows]) for r in rows]
    last = reordered(jnp.stack(last))
    moved, qkv_kept, last = tie(moved, qkv_kept, last)
    qkv_sums = finished(halves_of(jnp.concatenate(qkv_kept, axis=1)))
    input_rows = add_input(input_rows, moved, pairs - 1)
    last = trade(last)
    both_sum = add_blocks(last[:, :part_rows])
    inner_weight_grad, output_weight_grad = both_sum[:, :units], both_sum[:, units:]
    digit_rows = last[:, part_rows:, units:].astype(jnp.float32)
    query_bias_grad = (digit_rows[:, 0] + digit_rows[:, 1] + digit_rows[:, 2]).reshape(-1)
    qkv_sums = jnp.split(qkv_sums.astype(jnp.float32), 3 * pairs, axis=1)
    query_weight_grad, key_weight_grad, value_weight_grad = [
        jnp.concatenate(qkv_sums[i::3], axis=1) for i in range(3)
    ]

    wide = ranks * units // model_width
    inner_bias_grad = vectors[:wide].reshape(-1)
    (
        output_bias_grad,
        first_gain_grad,
        first_shift_grad,
        outer_bias_grad,
        second_gain_grad,
        second_shift_grad,
        value_bias_grad,
    ) = [vectors[wide + i] for i in range(7)]
    return (
        final.astype(jnp.bfloat16),
        vectors[wide + 7, 0] / token_total,
        input_rows,
        query_weight_grad,
        query_bias_grad,
        key_weight_grad,
        value_weight_grad,
        value_bias_grad,
        output_weight_grad,
        output_bias_grad,
        first_gain_grad,
        first_shift_grad,
        inner_weight_grad,
        inner_bias_grad,
        outer_weight_grad,
        outer_bias_grad,
        second_gain_grad,
        second_shift_grad,
    )


def solution(mesh):
    rows, columns, split = P("dp", None), P(None, "tensor"), P("dp", "tensor")
    part, whole, own = P("tensor"), P(), P(("dp", "tensor"), None)
    in_specs = (
        rows,
        P("dp"),
        columns,
        part,
        columns,
        columns,
        part,
        columns,
        whole,
        whole,
        whole,
        columns,
        part,
        columns,
        whole,
        whole,
        whole,
        rows,
        rows,
    )
    out_specs = (
        own,
        whole,
        own,
        split,
        whole,
        split,
        split,
        whole,
        split,
        whole,
        whole,
        whole,
        split,
        whole,
        split,
        whole,
        whole,
        whole,
    )
    return jax.shard_map(shards, mesh=mesh, in_specs=in_specs, out_specs=out_specs, check_vma=False)
```

profile of v0, /device:TPU:0, one launch (start us, length us, event | category | flops | bytes accessed | tf_op | source)
XLA Modules:
  0.0 442.9 jit_solution(18375238096253099980)
XLA Ops:
  9.6 6.3 %all-to-all-start = ((bf16[4,136,256]{2,1,0:T(8,128)(2,1)}), bf16[4,136,256]{2,1,0:T(8,128)(2,1)S(1)}, u32[]{:S(2)}, u32[]{:S(2)}) async-start(bf16[4,136,256]{2,1,0:T(8,128)(2,1)} %broadcast_in_dim.31), calls=%async_computation | async-start | bytes 557056 | tf_op jit(solution)/shard_map/all_to_all | solution.py:306
  24.9 4.7 %fusion.15.q_ref.k_ref.v_ref = bf16[2048,768]{1,0:T(8,128)(2,1)} fusion(f32[768]{0:T(1024)S(1)} %convert_element_type.389, bf16[2048,1024]{1,0:T(8,128)(2,1)S(1)} %copy-done.11, bf16[1024,768]{1,0:T(8,128)(2,1)S(1)} %get-tuple-element.184), kind=kOutput, calls=%fused_computation.27 | convolution fusion | flops 3224371200 | bytes 8915968 | tf_op jit(solution)/shard_map/dot_general | solution.py:17
  30.3 4.1 collective-permute-done
  37.8 31.1 %attend_forward.1 = (bf16[2048,256]{1,0:T(8,128)(2,1)}, bf16[4,2048,128]{2,1,0:T(8,128)(2,1)}) custom-call(s32[1]{0:T(128)} %copy.74.length_ref, bf16[2048,768]{1,0:T(8,128)(2,1)} %fusion.15.q_ref.k_ref.v_ref, bf16[2048,768]{1,0:T(8,128)(2,1)} %fusion.15.q_ref.k_ref.v_ref, bf16[2048,768]{1,0:T(8,128)(2,1)} %fusion.15.q_ref.k_ref.v_ref), custom_call_target="tpu_custom_call" | custom-call | flops 17179869184 | bytes 6291456 | tf_op jit(solution)/shard_map/attend_forward/pallas_call | solution.py:115
  72.9 14.3 %all-to-all-start.1 = ((bf16[4,512,256]{2,1,0:T(8,128)(2,1)}), bf16[4,512,256]{2,1,0:T(8,128)(2,1)S(1)}, u32[]{:S(2)}, u32[]{:S(2)}) async-start(bf16[4,512,256]{2,1,0:T(8,128)(2,1)} %bitcast.1), calls=%async_computation.1 | async-start | bytes 2097152 | tf_op jit(solution)/shard_map/all_to_all | solution.py:306
  94.6 18.4 %all-to-all-done.1 = bf16[4,512,256]{2,1,0:T(8,128)(2,1)S(1)} async-done(((bf16[4,512,256]{2,1,0:T(8,128)(2,1)}), bf16[4,512,256]{2,1,0:T(8,128)(2,1)S(1)}, u32[]{:S(2)}, u32[]{:S(2)}) %all-to-all-start.1) | async-done | bytes 1048608 | tf_op jit(solution)/shard_map/all_to_all | solution.py:306
  130.1 7.8 %all-gather.6.cloned.1.call-done = bf16[2,1024,2048]{2,1,0:T(8,128)(2,1)} async-done(((bf16[2,128,2048]{2,1,0:T(8,128)(2,1)}), bf16[2,1024,2048]{2,1,0:T(8,128)(2,1)}) %all-gather.6.cloned.1.call-update) | async-done | bytes 8388624 | tf_op jit(solution)/shard_map/all_gather | solution.py:303
  153.7 5.4 %multiply_reduce_fusion = (f32[1024]{0:T(1024)S(1)}, f32[512]{0:T(512)S(1)}, f32[]{:T(128)}, f32[512]{0:T(512)S(1)}, f32[1024]{0:T(1024)S(1)}, /*index=5*/f32[512,1024]{1,0:T(8,128)S(1)}, bf16[512,1024]{1,0:T(8,128)(2,1)}) fusion(f32[512]{0:T(512)S(1)} %add_rsqrt_fusion, f32[512,1024]{1,0:T(8,128)S(1)} %get-tuple-element.240, ...), kind=kLoop, calls=%fused_computation.56 | loop fusion | flops 11006975 | bytes 7365132 | tf_op jit(solution)/shard_map/reduce_sum | solution.py:390
  161.7 7.5 %convolution_convert_fusion.1 = bf16[1024,4096]{1,0:T(8,128)(2,1)} fusion(bf16[512,1024]{1,0:T(8,128)(2,1)S(1)} %fusion.127, bf16[512,1024]{1,0:T(8,128)(2,1)S(1)} %get-tuple-element.231, bf16[512,1024]{1,0:T(8,128)(2,1)S(1)} %get-tuple-element.233, bf16[512,1024]{1,0:T(8,128)(2,1)S(1)} %copy-done.66, bf16[512,1024]{1,0:T(8,128)(2,1)S(1)} %copy-done.61), kind=kOutput, calls=%fused_computation.3 | convolution fusion | flops 4315938816 | bytes 13631488 | tf_op jit(solution)/shard_map/dot_general | solution.py:27
  173.6 4.8 %multiply_convert_fusion = bf16[512,1024]{1,0:T(8,128)(2,1)} fusion(bf16[512,1024]{1,0:T(8,128)(2,1)S(1)} %fusion.127, bf16[1024,2048]{1,0:T(8,128)(2,1)} %copy-done.18, f32[512,1024]{1,0:T(8,128)} %get-tuple-element.232, f32[1024]{0:T(1024)S(1)} %bitcast.249), kind=kOutput, calls=%fused_computation.66 | convolution fusion | flops 1080557568 | bytes 6295552 | tf_op jit(solution)/shard_map/dot_general | solution.py:17
  205.0 6.5 %convolution_convert_fusion = bf16[1024,4096]{1,0:T(8,128)(2,1)S(1)} fusion(bf16[512,1024]{1,0:T(8,128)(2,1)S(1)} %copy-done.35, bf16[512,1024]{1,0:T(8,128)(2,1)} %multiply_convert_fusion, bf16[512,1024]{1,0:T(8,128)(2,1)} %multiply_convert_fusion.1, bf16[512,1024]{1,0:T(8,128)(2,1)} %copy-done.39, bf16[512,1024]{1,0:T(8,128)(2,1)S(1)} %multiply_convert_fusion.3), kind=kOutput, calls=%fused_computation.2 | convolution fusion | flops 4315938816 | bytes 13631488 | tf_op jit(solution)/shard_map/dot_general | solution.py:27
  211.5 4.0 constant_dynamic-slice_fusion.19
  219.6 4.4 all-to-all-start.2
  228.9 7.4 %fusion = bf16[512,4096]{1,0:T(8,128)(2,1)} fusion(bf16[512,4096]{1,0:T(8,128)(2,1)} %collective-permute-done.6, bf16[4,1,128,4096]{3,2,1,0:T(8,128)(2,1)} %get-tuple-element.122), kind=kLoop, calls=%fused_computation.1 | loop fusion | flops 8388608 | bytes 12582912 | tf_op jit(solution)/shard_map/convert_element_type | solution.py:346
  236.3 14.0 %all-to-all-done.2 = bf16[4,512,256]{2,1,0:T(8,128)(2,1)S(1)} async-done(((bf16[4,512,256]{2,1,0:T(8,128)(2,1)}), bf16[4,512,256]{2,1,0:T(8,128)(2,1)S(1)}, u32[]{:S(2)}, u32[]{:S(2)}) %all-to-all-start.2) | async-done | bytes 1048608 | tf_op jit(solution)/shard_map/all_to_all | solution.py:306
  260.9 4.3 all-to-all-start.3
  265.2 28.9 %attend_backward.2 = bf16[2048,384]{1,0:T(8,128)(2,1)} custom-call(s32[1]{0:T(128)} %copy.74.length_ref, bf16[4,2048,128]{2,1,0:T(8,128)(2,1)} %get-tuple-element.80.extended_ref, bf16[2048,768]{1,0:T(8,128)(2,1)} %fusion.15.q_ref.k_ref.v_ref, bf16[2048,768]{1,0:T(8,128)(2,1)} %fusion.15.q_ref.k_ref.v_ref, bf16[2048,256]{1,0:T(8,128)(2,1)} %get-tuple-element.81.context_ref, ...), custom_call_target="tpu_custom_call" | custom-call | flops 21474836480 | bytes 5242880 | tf_op jit(solution)/shard_map/attend_backward/pallas_call | solution.py:208
  294.1 5.4 %all-to-all-start.4 = ((bf16[4,512,384]{2,1,0:T(8,128)(2,1)}), bf16[4,512,384]{2,1,0:T(8,128)(2,1)}, u32[]{:S(2)}, u32[]{:S(2)}) async-start(bf16[4,512,384]{2,1,0:T(8,128)(2,1)} %bitcast.206), calls=%async_computation.5 | async-start | bytes 3145728 | tf_op jit(solution)/shard_map/all_to_all | solution.py:306
  317.3 28.8 %attend_backward.3 = bf16[2048,384]{1,0:T(8,128)(2,1)} custom-call(s32[1]{0:T(128)} %copy.74.length_ref, bf16[4,2048,128]{2,1,0:T(8,128)(2,1)} %get-tuple-element.80.extended_ref, bf16[2048,768]{1,0:T(8,128)(2,1)} %fusion.15.q_ref.k_ref.v_ref, bf16[2048,768]{1,0:T(8,128)(2,1)} %fusion.15.q_ref.k_ref.v_ref, bf16[2048,256]{1,0:T(8,128)(2,1)} %get-tuple-element.81.context_ref, ...), custom_call_target="tpu_custom_call" | custom-call | flops 21474836480 | bytes 5242880 | tf_op jit(solution)/shard_map/attend_backward/pallas_call | solution.py:208
  346.2 4.1 convolution_convert_fusion.4
  351.6 4.6 %all-to-all-start.5 = ((bf16[4,512,384]{2,1,0:T(8,128)(2,1)}), bf16[4,512,384]{2,1,0:T(8,128)(2,1)}, u32[]{:S(2)}, u32[]{:S(2)}) async-start(bf16[4,512,384]{2,1,0:T(8,128)(2,1)} %bitcast.205), calls=%async_computation.7 | async-start | bytes 3145728 | tf_op jit(solution)/shard_map/all_to_all | solution.py:306
  384.0 9.5 %all-to-all-done.5 = bf16[4,512,384]{2,1,0:T(8,128)(2,1)} async-done(((bf16[4,512,384]{2,1,0:T(8,128)(2,1)}), bf16[4,512,384]{2,1,0:T(8,128)(2,1)}, u32[]{:S(2)}, u32[]{:S(2)}) %all-to-all-start.5) | async-done | bytes 1572896 | tf_op jit(solution)/shard_map/all_to_all | solution.py:306
  403.7 6.2 %add_add_fusion = f32[512,1024]{1,0:T(8,128)} fusion(f32[512,1024]{1,0:T(8,128)S(1)} %copy-done.22, f32[512,1024]{1,0:T(8,128)} %fusion.62, bf16[1024,1536]{1,0:T(8,128)(2,1)} %copy-done.48, bf16[512,384]{1,0:T(8,128)(2,1)} %get-tuple-element.145, bf16[512,384]{1,0:T(8,128)(2,1)} %get-tuple-element.146, bf16[512,384]{1,0:T(8,128)(2,1)} %get-tuple-element.147, ...), kind=kOutput, calls=%fused_computation.51 | convolution fusion | flops 1617952768 | bytes 11010048 | tf_op jit(solution)/shard_map/dot_general | solution.py:21
  418.6 13.8 %all-to-all-done.6 = bf16[4,136,1280]{2,1,0:T(8,128)(2,1)S(1)} async-done(((bf16[4,136,1280]{2,1,0:T(8,128)(2,1)}), bf16[4,136,1280]{2,1,0:T(8,128)(2,1)S(1)}, u32[]{:S(2)}, u32[]{:S(2)}) %all-to-all-start.6) | async-done | bytes 1392672 | tf_op jit(solution)/shard_map/all_to_all | solution.py:306
  (374 shorter events, 176.9 us)
Async XLA Ops:
  9.6 20.7 %all-to-all-start = ((bf16[4,136,256]{2,1,0:T(8,128)(2,1)}), bf16[4,136,256]{2,1,0:T(8,128)(2,1)S(1)}, u32[]{:S(2)}, u32[]{:S(2)}) async-start(bf16[4,136,256]{2,1,0:T(8,128)(2,1)} %broadcast_in_dim.31), calls=%async_computation | async-start | bytes 557056 | tf_op jit(solution)/shard_map/all_to_all | solution.py:306
  16.0 97.1 %all-gather.4.cloned.1.call-start = ((), (), s32[]{:S(2)}) async-start(), calls=%async_computation.9 | async-start | bytes 6782976 | tf_op jit(solution)/shard_map/all_gather | solution.py:412
  35.5 102.4 %all-gather.6.cloned.1.call-start = ((), (), s32[]{:S(2)}) async-start(), calls=%async_computation.10 | async-start | bytes 9437184 | tf_op jit(solution)/shard_map/all_gather | solution.py:303
  35.5 36.3 %collective-permute-start.1 = (bf16[128,2048]{1,0:T(8,128)(2,1)S(1)}, bf16[128,2048]{1,0:T(8,128)(2,1)S(1)}, u32[]{:S(2)}, u32[]{:S(2)}) collective-permute-start(bf16[128,2048]{1,0:T(8,128)(2,1)S(1)} %fusion.92), channel_id=1, source_target_pairs={{0,2},{1,3},{2,0},{3,1},{4,6},{5,7},{6,4},{7,5},{8,10},{9,11},{10,... | collective-permute-start | bytes 1572872 | tf_op jit(solution)/shard_map/ppermute | solution.py:243
  37.6 34.2 %collective-permute-start.2 = (bf16[128,2048]{1,0:T(8,128)(2,1)S(1)}, bf16[128,2048]{1,0:T(8,128)(2,1)S(1)}, u32[]{:S(2)}, u32[]{:S(2)}) collective-permute-start(bf16[128,2048]{1,0:T(8,128)(2,1)S(1)} %fusion.92), channel_id=1, source_target_pairs={{0,3},{1,2},{2,1},{3,0},{4,7},{5,6},{6,5},{7,4},{8,11},{9,10},{10,... | collective-permute-start | bytes 1572872 | tf_op jit(solution)/shard_map/ppermute | solution.py:243
  72.9 40.1 %all-to-all-start.1 = ((bf16[4,512,256]{2,1,0:T(8,128)(2,1)}), bf16[4,512,256]{2,1,0:T(8,128)(2,1)S(1)}, u32[]{:S(2)}, u32[]{:S(2)}) async-start(bf16[4,512,256]{2,1,0:T(8,128)(2,1)} %bitcast.1), calls=%async_computation.1 | async-start | bytes 2097152 | tf_op jit(solution)/shard_map/all_to_all | solution.py:306
  87.2 171.3 %reduce-scatter.3.cloned.1.call-start = ((), (), s32[]{:S(2)}) async-start(), calls=%async_computation.11 | async-start | bytes 9437184 | tf_op jit(solution)/shard_map/reduce_scatter | solution.py:387
  169.2 33.8 %collective-permute-start.5 = (bf16[128,768]{1,0:T(8,128)(2,1)}, bf16[128,768]{1,0:T(8,128)(2,1)}, u32[]{:S(2)}, u32[]{:S(2)}) collective-permute-start(bf16[128,768]{1,0:T(8,128)(2,1)} %constant_dynamic-slice_fusion.20), channel_id=1, source_target_pairs={{0,3},{1,2},{2,1},{3,0},{4,7},{5,6},{6,5},{7,4},{8,11},{9,10},{10,... | collective-permute-start | bytes 589832 | tf_op jit(solution)/shard_map/ppermute | solution.py:243
  172.5 30.4 %collective-permute-start.4 = (bf16[128,768]{1,0:T(8,128)(2,1)}, bf16[128,768]{1,0:T(8,128)(2,1)}, u32[]{:S(2)}, u32[]{:S(2)}) collective-permute-start(bf16[128,768]{1,0:T(8,128)(2,1)} %constant_dynamic-slice_fusion.20), channel_id=1, source_target_pairs={{0,2},{1,3},{2,0},{3,1},{4,6},{5,7},{6,4},{7,5},{8,10},{9,11},{10,... | collective-permute-start | bytes 589832 | tf_op jit(solution)/shard_map/ppermute | solution.py:243
  172.5 30.4 %collective-permute-start.3 = (bf16[128,768]{1,0:T(8,128)(2,1)}, bf16[128,768]{1,0:T(8,128)(2,1)}, u32[]{:S(2)}, u32[]{:S(2)}) collective-permute-start(bf16[128,768]{1,0:T(8,128)(2,1)} %constant_dynamic-slice_fusion.20), channel_id=1, source_target_pairs={{0,1},{1,0},{2,3},{3,2},{4,5},{5,4},{6,7},{7,6},{8,9},{9,8},{10,11... | collective-permute-start | bytes 589832 | tf_op jit(solution)/shard_map/ppermute | solution.py:243
  219.6 30.6 %all-to-all-start.2 = ((bf16[4,512,256]{2,1,0:T(8,128)(2,1)}), bf16[4,512,256]{2,1,0:T(8,128)(2,1)S(1)}, u32[]{:S(2)}, u32[]{:S(2)}) async-start(bf16[4,512,256]{2,1,0:T(8,128)(2,1)} %pad_maximum_fusion.7), calls=%async_computation.2 | async-start | bytes 2097152 | tf_op jit(solution)/shard_map/all_to_all | solution.py:306
  224.0 122.1 %reduce-scatter.5.cloned.1.call-start = ((), (), s32[]{:S(2)}) async-start(), calls=%async_computation.12 | async-start | bytes 2359296 | tf_op jit(solution)/shard_map/reduce_scatter | solution.py:387
  250.2 95.9 %all-gather.8.cloned.1.call-start = ((), (), s32[]{:S(2)}) async-start(), calls=%async_computation.13 | async-start | bytes 5308416 | tf_op jit(solution)/shard_map/all_gather | solution.py:303
  250.9 43.2 %collective-permute-start.10 = (f32[12,1024]{1,0:T(8,128)S(1)}, f32[12,1024]{1,0:T(8,128)S(1)}, u32[]{:S(2)}, u32[]{:S(2)}) collective-permute-start(f32[12,1024]{1,0:T(8,128)S(1)} %add.425), channel_id=1, source_target_pairs={{0,1},{1,0},{2,3},{3,2},{4,5},{5,4},{6,7},{7,6},{8,9},{9,8},{10,11... | collective-permute-start | bytes 147464 | tf_op jit(solution)/shard_map/ppermute | solution.py:243
  254.9 39.2 %collective-permute-start.9 = (bf16[2,1,128,2048]{3,2,1,0:T(8,128)(2,1)}, bf16[2,1,128,2048]{3,2,1,0:T(8,128)(2,1)}, u32[]{:S(2)}, u32[]{:S(2)}) collective-permute-start(bf16[2,1,128,2048]{3,2,1,0:T(8,128)(2,1)} %get-tuple-element.140), channel_id=1, source_target_pairs={{0,8},{4,12},{8,0},{12,4},{16,24},{20,28},{24,16},{28,20},{1,9},{5... | collective-permute-start | bytes 3145736 | tf_op jit(solution)/shard_map/ppermute | solution.py:243
  258.1 36.1 %collective-permute-start.8 = (bf16[1,2,128,2048]{3,2,1,0:T(8,128)(2,1)}, bf16[1,2,128,2048]{3,2,1,0:T(8,128)(2,1)}, u32[]{:S(2)}, u32[]{:S(2)}) collective-permute-start(bf16[1,2,128,2048]{3,2,1,0:T(8,128)(2,1)} %get-tuple-element.142), channel_id=1, source_target_pairs={{0,16},{4,20},{8,24},{12,28},{16,0},{20,4},{24,8},{28,12},{1,17},{... | collective-permute-start | bytes 3145736 | tf_op jit(solution)/shard_map/ppermute | solution.py:243
  260.9 33.2 %all-to-all-start.3 = ((bf16[4,128,1024]{2,1,0:T(8,128)(2,1)}), bf16[4,128,1024]{2,1,0:T(8,128)(2,1)}, u32[]{:S(2)}, u32[]{:S(2)}) async-start(bf16[4,128,1024]{2,1,0:T(8,128)(2,1)} %pad_maximum_fusion.8), calls=%async_computation.4 | async-start | bytes 2097152 | tf_op jit(solution)/shard_map/all_to_all | solution.py:306
  294.1 52.0 %all-to-all-start.4 = ((bf16[4,512,384]{2,1,0:T(8,128)(2,1)}), bf16[4,512,384]{2,1,0:T(8,128)(2,1)}, u32[]{:S(2)}, u32[]{:S(2)}) async-start(bf16[4,512,384]{2,1,0:T(8,128)(2,1)} %bitcast.206), calls=%async_computation.5 | async-start | bytes 3145728 | tf_op jit(solution)/shard_map/all_to_all | solution.py:306
  299.6 46.5 %collective-permute-start.14 = (f32[12,1024]{1,0:T(8,128)S(1)}, f32[12,1024]{1,0:T(8,128)S(1)}, u32[]{:S(2)}, u32[]{:S(2)}) collective-permute-start(f32[12,1024]{1,0:T(8,128)S(1)} %add.434), channel_id=1, source_target_pairs={{0,2},{1,3},{2,0},{3,1},{4,6},{5,7},{6,4},{7,5},{8,10},{9,11},{10,... | collective-permute-start | bytes 147464 | tf_op jit(solution)/shard_map/ppermute | solution.py:243
  308.1 38.0 %collective-permute-start.12 = (bf16[1,1,128,2048]{3,2,1,0:T(8,128)(2,1)}, bf16[1,1,128,2048]{3,2,1,0:T(8,128)(2,1)}, u32[]{:S(2)}, u32[]{:S(2)}) collective-permute-start(bf16[1,1,128,2048]{3,2,1,0:T(8,128)(2,1)} %get-tuple-element.164), channel_id=1, source_target_pairs={{0,8},{4,12},{8,0},{12,4},{16,24},{20,28},{24,16},{28,20},{1,9},{5... | collective-permute-start | bytes 1572872 | tf_op jit(solution)/shard_map/ppermute | solution.py:243
  311.7 34.5 %collective-permute-start.13 = (bf16[1,1,128,2048]{3,2,1,0:T(8,128)(2,1)}, bf16[1,1,128,2048]{3,2,1,0:T(8,128)(2,1)S(1)}, u32[]{:S(2)}, u32[]{:S(2)}) collective-permute-start(bf16[1,1,128,2048]{3,2,1,0:T(8,128)(2,1)} %get-tuple-element.162), channel_id=1, source_target_pairs={{0,16},{4,20},{8,24},{12,28},{16,0},{20,4},{24,8},{28,12},{1,17},{... | collective-permute-start | bytes 1572872 | tf_op jit(solution)/shard_map/ppermute | solution.py:243
  351.6 42.0 %all-to-all-start.5 = ((bf16[4,512,384]{2,1,0:T(8,128)(2,1)}), bf16[4,512,384]{2,1,0:T(8,128)(2,1)}, u32[]{:S(2)}, u32[]{:S(2)}) async-start(bf16[4,512,384]{2,1,0:T(8,128)(2,1)} %bitcast.205), calls=%async_computation.7 | async-start | bytes 3145728 | tf_op jit(solution)/shard_map/all_to_all | solution.py:306
  356.4 24.6 %collective-permute-start.18 = (bf16[512,384]{1,0:T(8,128)(2,1)}, bf16[512,384]{1,0:T(8,128)(2,1)}, u32[]{:S(2)}, u32[]{:S(2)}) collective-permute-start(bf16[512,384]{1,0:T(8,128)(2,1)} %convolution_convert_fusion.4), channel_id=1, source_target_pairs={{0,4},{4,0},{8,12},{12,8},{16,20},{20,16},{24,28},{28,24},{1,5},{5... | collective-permute-start | bytes 1179656 | tf_op jit(solution)/shard_map/ppermute | solution.py:243
  396.1 36.3 %all-to-all-start.6 = ((bf16[4,136,1280]{2,1,0:T(8,128)(2,1)}), bf16[4,136,1280]{2,1,0:T(8,128)(2,1)S(1)}, u32[]{:S(2)}, u32[]{:S(2)}) async-start(bf16[4,136,1280]{2,1,0:T(8,128)(2,1)} %pad_maximum_fusion.2), calls=%async_computation.8 | async-start | bytes 2785280 | tf_op jit(solution)/shard_map/all_to_all | solution.py:306
  (82 other events, 483.3 us)
Sparse Core Ops, SparseCore 0:
  35.6 43.9 all-gather.3
  82.1 55.7 all-gather.5
  181.3 71.4 reduce-scatter.2
  256.0 42.1 reduce-scatter.4
  299.9 44.9 all-gather.7
where the time goes:
time: 450 us; the launch traced here: 443 us
  Pallas kernels  88.8 us (20%)
  matrix products  87.4 us (19%)
  waiting for transfers between devices  81.3 us (18%)
  starting transfers between devices  66.8 us (15%)
  local copies, waits for them, and re-layouts  54.5 us (12%)
  other arithmetic  44.4 us (10%)
  between operations  19.6 us (4%)
    pallas_call x2, Pallas kernels, attend_backward(): pl.pallas_call(backward_kernel, grid_spec=pltpu.PrefetchScalarGridSpec(nu...  57.7 us
    all_to_all x7, waiting for transfers between devices, trade(): return lax.all_to_all(blocks, 'tensor', 0, 0)  55.7 us
    all_to_all x7, starting transfers between devices, trade(): return lax.all_to_all(blocks, 'tensor', 0, 0)  43 us
    dot_general x14, matrix products, matmul(): return jnp.dot(former, latter, preferred_element_type=jnp.float32)  41 us
    pallas_call x1, Pallas kernels, attend_forward(): pl.pallas_call(forward_kernel, grid_spec=pltpu.PrefetchScalarGridSpec(num...  31.1 us
    dot_general x11, matrix products, times_rows(): lax.dot_general(former, latter, (((1,), (1,)), ((), ())), preferred_eleme...  28.7 us
    ppermute x23, starting transfers between devices, flip(): lax.ppermute(array_in, axis_name, [(i, i ^ bits) for i in range(size)])  23.4 us
    dot_general x3, matrix products, over_rows(): lax.dot_general(former, latter, (((0,), (0,)), ((), ())), preferred_eleme...  17.8 us
  transfers between devices with their start and end apart: 35, of which 11 were waited for; matrix products, arithmetic and copies ran while one was open for 30% of the time, Pallas kernels for 20%

commit v1 on v0

--- a/solution.py
+++ b/solution.py
@@ -348,40 +348,18 @@
     def qkv_product(qkv_low):
         return [matmul(half, qkv_low).astype(jnp.bfloat16) for half in hidden_halves]
 
-    def halves_of(kept):
-        places = list(range(1, copies.bit_length() - 1))
-        states = []
-        for part, order in zip(jnp.split(kept, 2, axis=1), (places[::-1], places)):
-            states.append((part.reshape(copies // 2, -1, part.shape[1]), list(places), order))
-        return states
-
-    def begin(states):
-        started = []
-        for blocks, left, order in states:
-            place = order[0]
-            low = 2 ** sum(p < place for p in left)
-            split = blocks.reshape(-1, 2, low, *blocks.shape[1:])
-            mine = (copy >> place) & 1
-            keep = lax.dynamic_index_in_dim(split, mine, 1, keepdims=False)
-            give = lax.dynamic_index_in_dim(split, 1 - mine, 1, keepdims=False)
-            started.append((keep, flip(give, "dp", 1 << place)))
-        return started
-
-    def complete(states, started):
-        out = []
-        for (blocks, left, order), (keep, come) in zip(states, started):
-            added = keep.astype(jnp.float32) + come.astype(jnp.float32)
-            added = added.astype(jnp.bfloat16).reshape(-1, *blocks.shape[1:])
-            out.append((added, [p for p in left if p != order[0]], order[1:]))
-        return out
-
-    def step(states):
-        return complete(states, begin(states))
-
-    def finished(states):
-        while states[0][2]:
-            states = step(states)
-        return jnp.concatenate([blocks[0] for blocks, _, _ in states], axis=1)
+    def to_chips(kept):
+        blocks = [part.reshape(copies // 2, -1, part.shape[1]) for part in kept]
+        rows = []
+        for t in range(copies // 2):
+            pieces = [
+                lax.dynamic_index_in_dim(b, (copy >> 1) ^ t, 0, keepdims=False) for b in blocks
+            ]
+            rows.append(jnp.concatenate(pieces, axis=1))
+        return [rows[0]] + [flip(rows[t], "dp", 2 * t) for t in range(1, copies // 2)]
+
+    def add_all(parts):
+        return sum(part.astype(jnp.float32) for part in parts)
 
     def scatter_copies(whole):
         return lax.psum_scatter(whole, "dp", scatter_dimension=0, tiled=True)
@@ -415,7 +393,7 @@
     context, extended = attend_forward(lengths, qkv)
     received = trade(context.reshape(ranks, share_rows, heads_width))
     far_parts, context, hidden_late = tie(far_parts, context, hidden_in)
-    far_rows = gathered(jnp.stack(far_parts))
+    far_rows = gathered(jnp.stack([p[:, i : i + units] for p in far_parts for i in (0, units)]))
     hidden_halves = [half_columns(hidden_late, other).T for other in range(2)]
     received, hidden_halves = tie(received, hidden_halves)
     digits = near_rows[::part_rows, -PAIR:].astype(jnp.float32)
@@ -424,9 +402,11 @@
     context_all = jnp.concatenate(
         [block_of(received, s) for s in range(ranks)], axis=1
     )
-    both_rest = [near_rows[:, : 2 * units]] + [far_rows[i] for i in range(ranks - 2)]
-    inner_weights = [inner_weight] + [rest[:, :units] for rest in both_rest]
-    outer_weights = [outer_weight] + [rest[:, units:] for rest in both_rest]
+    inner_weights = [inner_weight, near_rows[:, :units]]
+    outer_weights = [outer_weight, near_rows[:, units : 2 * units]]
+    for i in range(ranks - 2):
+        inner_weights.append(far_rows[2 * i])
+        outer_weights.append(far_rows[2 * i + 1])
     inner_biases = [inner_bias] + [b.reshape(-1) for b in biases]
     output_weight_all = jnp.concatenate([output_weight, near_rows[:, 2 * units : -PAIR]], axis=1)
 
@@ -466,13 +446,14 @@
     attention_low = first_grad.astype(jnp.bfloat16)
     grad_all = matmul(attention_low, output_weight_all).astype(jnp.bfloat16)
     grad_all, inner_lows, qkv_parts = tie(grad_all, inner_lows, qkv_parts)
-    qkv_rest = gathered(qkv_parts)
     context_grad = trade(column_blocks(grad_all)).reshape(seq_len, heads_width)
     inner_whole = over_rows(normed_low, jnp.concatenate(inner_lows, axis=1)).astype(jnp.bfloat16)
-    inner_kept = with_other_core(half_rows(inner_whole, 0), half_rows(inner_whole, 1))
+    inner_kept = [
+        with_other_core(half_rows(half, 0), half_rows(half, 1))
+        for half in jnp.split(inner_whole, 2, axis=1)
+    ]
     output_whole = over_rows(attention_low, context_all).astype(jnp.bfloat16)
-    inner_states = halves_of(inner_kept)
-    inner_started = begin(inner_states)
+    inner_chips = to_chips(inner_kept)
     vectors = [
         ordered(jnp.concatenate([column_sums(low) for low in inner_lows])),
         column_sums(attention_low),
@@ -486,11 +467,11 @@
     ]
     vectors = jnp.concatenate([v.reshape(-1, model_width) for v in vectors])
     vectors = vectors + flip(vectors, "dp", 1)
-    context_grad, inner_kept, vectors, output_whole = tie(
-        context_grad, inner_kept, vectors, output_whole
-    )
-    output_rows = scatter_copies(output_whole)
-    outer_come = trade(column_blocks(outer_rows))
+    outer_blocks = column_blocks(outer_rows)
+    context_grad, vectors, output_whole, outer_blocks = tie(
+        context_grad, vectors, output_whole, outer_blocks
+    )
+    outer_come = trade(outer_blocks)
     rank_bits = [1 << p for p in range(ranks.bit_length() - 1)]
     vector_come = flip(vectors, "tensor", rank_bits[0])
 
@@ -505,28 +486,28 @@
     for pair in range(pairs):
         qkv_low = attend_backward(lengths, extended, qkv, context, context_grad, pair)
         if pair == 0:
-            qkv_low, inner_started, outer_come, vector_come = tie(
-                qkv_low, inner_started, outer_come, vector_come
+            qkv_low, inner_chips, outer_come, vector_come, qkv_parts, output_whole = tie(
+                qkv_low, inner_chips, outer_come, vector_come, qkv_parts, output_whole
             )
-            outer_weight_grad = add_blocks(outer_come)
-            inner_states = complete(inner_states, inner_started)
-            inner_started = begin(inner_states) if inner_states[0][2] else None
+            output_rows = scatter_copies(output_whole)
+            qkv_rest = gathered(qkv_parts)
+            inner_rows = add_all(inner_chips).astype(jnp.bfloat16)
+            inner_parts = jnp.split(inner_rows, ranks, axis=1)
             vectors = vectors + vector_come
             vector_come = flip(vectors, "tensor", rank_bits[1])
         if pair == 0:
             qkv_kept = [with_other_core(*qkv_product(qkv_low))]
-            context_grad, qkv_kept = tie(context_grad, qkv_kept)
+            context_grad, qkv_kept, inner_parts = tie(context_grad, qkv_kept, inner_parts)
+            inner_come = [flip(inner_parts[t], "tensor", t) for t in range(1, ranks)]
         else:
-            moved, qkv_low, inner_started, vector_come, output_rows, qkv_rest = tie(
-                moved, qkv_low, inner_started, vector_come, output_rows, qkv_rest
+            moved, qkv_low, inner_come, vector_come, output_rows, qkv_kept = tie(
+                moved, qkv_low, inner_come, vector_come, output_rows, qkv_kept
             )
             vectors = vectors + vector_come
             input_rows = add_input(input_rows, moved, pair - 1)
             qkv_kept.append(with_other_core(*qkv_product(qkv_low)))
         moved = trade(qkv_low.reshape(ranks, share_rows, -1))
         query_sums.append(column_sums(qkv_low[:, :PAIR]))
-    inner_states = complete(inner_states, inner_started)
-    inner_parts = finished(inner_states)
     if pairs == 1:
         vectors = vectors + vector_come
     for bit in rank_bits[2:]:
@@ -543,20 +524,19 @@
     middle = (query_sums - high.astype(jnp.float32)).astype(jnp.bfloat16)
     low = query_sums - high.astype(jnp.float32) - middle.astype(jnp.float32)
     digit_rows = jnp.stack([high, middle, low.astype(jnp.bfloat16)])
-    digit_rows = jnp.pad(digit_rows, ((0, 5), (units, 0)))
-    rows = [inner_parts, output_rows]
-    rows = [[jnp.split(r, ranks, axis=1)[s] for r in rows] for s in range(ranks)]
-    last = [jnp.concatenate([jnp.concatenate(r, axis=1), digit_rows]) for r in rows]
+    digit_rows = jnp.pad(digit_rows, ((0, 5), (0, 0)))
+    last = [jnp.concatenate([part, digit_rows]) for part in jnp.split(output_rows, ranks, axis=1)]
     last = reordered(jnp.stack(last))
-    moved, qkv_kept, last = tie(moved, qkv_kept, last)
-    qkv_sums = finished(halves_of(jnp.concatenate(qkv_kept, axis=1)))
+    moved, last, outer_come, inner_come = tie(moved, last, outer_come, inner_come)
+    outer_weight_grad = add_blocks(outer_come)
+    inner_weight_grad = add_all([inner_parts[0], *inner_come])
+    qkv_sums = add_all(to_chips(qkv_kept))
     input_rows = add_input(input_rows, moved, pairs - 1)
     last = trade(last)
-    both_sum = add_blocks(last[:, :part_rows])
-    inner_weight_grad, output_weight_grad = both_sum[:, :units], both_sum[:, units:]
-    digit_rows = last[:, part_rows:, units:].astype(jnp.float32)
+    output_weight_grad = add_blocks(last[:, :part_rows])
+    digit_rows = last[:, part_rows:].astype(jnp.float32)
     query_bias_grad = (digit_rows[:, 0] + digit_rows[:, 1] + digit_rows[:, 2]).reshape(-1)
-    qkv_sums = jnp.split(qkv_sums.astype(jnp.float32), 3 * pairs, axis=1)
+    qkv_sums = jnp.split(qkv_sums, 3 * pairs, axis=1)
     query_weight_grad, key_weight_grad, value_weight_grad = [
         jnp.concatenate(qkv_sums[i::3], axis=1) for i in range(3)
     ]

time: 450 us -> 435 us (0.967)
  waiting for transfers between devices: 81.3 us -> 69.3 us
  local copies, waits for them, and re-layouts: 54.5 us -> 45.3 us
  starting transfers between devices: 66.8 us -> 74.3 us
  matrix products: 87.4 us -> 82.9 us
    all_to_all x7, waiting for transfers between devices: 55.7 us -> 28.4 us  [trade(): return lax.all_to_all(blocks, 'tensor', 0, 0)]
    ppermute x23 -> x25, waiting for transfers between devices: 17.2 us -> 28.4 us  [flip(): lax.ppermute(array_in, axis_name, [(i, i ^ bits) for i in range(size)])]
    squeeze x9 -> x4, local copies, waits for them, and re-layouts: 10.7 us -> 0.58 us  [to_chips(): lax.dynamic_index_in_dim(b, copy >> 1 ^ t, 0, keepdims=False)]
    dot_general x11, matrix products: 28.7 us -> 22.1 us  [times_rows(): lax.dot_general(former, latter, (((1,), (1,)), ((), ())), preferred_eleme...]
    ppermute x23 -> x25, starting transfers between devices: 23.4 us -> 29.3 us  [flip(): lax.ppermute(array_in, axis_name, [(i, i ^ bits) for i in range(size)])]
    reduce_scatter x2, waiting for transfers between devices: 0.01 us -> 4.56 us  [scatter_copies(): return lax.psum_scatter(whole, 'dp', scatter_dimension=0, tiled=True)]
    unnamed x164 -> x166, local copies, waits for them, and re-layouts: 17.6 us -> 20.8 us
  transfers between devices with their start and end apart: 35 -> 37, of which waited for: 11 -> 15; matrix products, arithmetic and copies ran while one was open for 30% -> 29% of each run, Pallas kernels for 20% -> 21%
where the time goes in v1:
time: 435 us; the launch traced here: 428 us
  Pallas kernels  88.7 us (20%)
  matrix products  82.9 us (19%)
  starting transfers between devices  74.3 us (17%)
  waiting for transfers between devices  69.3 us (16%)
  other arithmetic  47.9 us (11%)
  local copies, waits for them, and re-layouts  45.3 us (10%)
  between operations  19.6 us (5%)
    pallas_call x2, Pallas kernels, attend_backward(): pl.pallas_call(backward_kernel, grid_spec=pltpu.PrefetchScalarGridSpec(nu...  57.6 us
    all_to_all x7, starting transfers between devices, trade(): return lax.all_to_all(blocks, 'tensor', 0, 0)  44.6 us
    dot_general x14, matrix products, matmul(): return jnp.dot(former, latter, preferred_element_type=jnp.float32)  43.8 us
    pallas_call x1, Pallas kernels, attend_forward(): pl.pallas_call(forward_kernel, grid_spec=pltpu.PrefetchScalarGridSpec(num...  31.1 us
    ppermute x25, starting transfers between devices, flip(): lax.ppermute(array_in, axis_name, [(i, i ^ bits) for i in range(size)])  29.3 us
    ppermute x25, waiting for transfers between devices, flip(): lax.ppermute(array_in, axis_name, [(i, i ^ bits) for i in range(size)])  28.4 us
    all_to_all x7, waiting for transfers between devices, trade(): return lax.all_to_all(blocks, 'tensor', 0, 0)  28.4 us
    dot_general x11, matrix products, times_rows(): lax.dot_general(former, latter, (((1,), (1,)), ((), ())), preferred_eleme...  22.1 us
  transfers between devices with their start and end apart: 37, of which 15 were waited for; matrix products, arithmetic and copies ran while one was open for 29% of the time, Pallas kernels for 21%

profile of v1, /device:TPU:0, one launch (start us, length us, event | category | flops | bytes accessed | tf_op | source)
XLA Modules:
  0.0 428.1 jit_solution(17106510730503466968)
XLA Ops:
  9.6 6.3 %all-to-all-start = ((bf16[4,136,256]{2,1,0:T(8,128)(2,1)}), bf16[4,136,256]{2,1,0:T(8,128)(2,1)S(1)}, u32[]{:S(2)}, u32[]{:S(2)}) async-start(bf16[4,136,256]{2,1,0:T(8,128)(2,1)} %broadcast_in_dim.31), calls=%async_computation | async-start | bytes 557056 | tf_op jit(solution)/shard_map/all_to_all | solution.py:306
  24.9 4.7 %fusion.16.q_ref.k_ref.v_ref = bf16[2048,768]{1,0:T(8,128)(2,1)} fusion(f32[768]{0:T(1024)S(1)} %convert_element_type.339, bf16[2048,1024]{1,0:T(8,128)(2,1)S(1)} %copy-done.12, bf16[1024,768]{1,0:T(8,128)(2,1)S(1)} %get-tuple-element.196), kind=kOutput, calls=%fused_computation.27 | convolution fusion | flops 3224371200 | bytes 8915968 | tf_op jit(solution)/shard_map/dot_general | solution.py:17
  30.3 4.1 collective-permute-done
  37.8 31.1 %attend_forward.1 = (bf16[2048,256]{1,0:T(8,128)(2,1)}, bf16[4,2048,128]{2,1,0:T(8,128)(2,1)}) custom-call(s32[1]{0:T(128)} %copy.70.length_ref, bf16[2048,768]{1,0:T(8,128)(2,1)} %fusion.16.q_ref.k_ref.v_ref, bf16[2048,768]{1,0:T(8,128)(2,1)} %fusion.16.q_ref.k_ref.v_ref, bf16[2048,768]{1,0:T(8,128)(2,1)} %fusion.16.q_ref.k_ref.v_ref), custom_call_target="tpu_custom_call" | custom-call | flops 17179869184 | bytes 6291456 | tf_op jit(solution)/shard_map/attend_forward/pallas_call | solution.py:115
  73.0 14.3 %all-to-all-start.1 = ((bf16[4,512,256]{2,1,0:T(8,128)(2,1)}), bf16[4,512,256]{2,1,0:T(8,128)(2,1)S(1)}, u32[]{:S(2)}, u32[]{:S(2)}) async-start(bf16[4,512,256]{2,1,0:T(8,128)(2,1)} %bitcast.1), calls=%async_computation.1 | async-start | bytes 2097152 | tf_op jit(solution)/shard_map/all_to_all | solution.py:306
  94.8 18.4 %all-to-all-done.1 = bf16[4,512,256]{2,1,0:T(8,128)(2,1)S(1)} async-done(((bf16[4,512,256]{2,1,0:T(8,128)(2,1)}), bf16[4,512,256]{2,1,0:T(8,128)(2,1)S(1)}, u32[]{:S(2)}, u32[]{:S(2)}) %all-to-all-start.1) | async-done | bytes 1048608 | tf_op jit(solution)/shard_map/all_to_all | solution.py:306
  130.2 7.8 %all-gather.6.cloned.1.call-done = bf16[4,1024,1024]{2,1,0:T(8,128)(2,1)} async-done(((bf16[4,128,1024]{2,1,0:T(8,128)(2,1)}), bf16[4,1024,1024]{2,1,0:T(8,128)(2,1)}) %all-gather.6.cloned.1.call-update) | async-done | bytes 8388624 | tf_op jit(solution)/shard_map/all_gather | solution.py:303
  138.0 4.4 %multiply_convert_fusion.4 = (bf16[512,1024]{1,0:T(8,128)(2,1)S(1)}, f32[512,1024]{1,0:T(8,128)}) fusion(f32[1024]{0:T(1024)S(1)} %bitcast.277, bf16[512,1024]{1,0:T(8,128)(2,1)S(1)} %fusion.37, bf16[4,1024,1024]{2,1,0:T(8,128)(2,1)} %all-gather.6.cloned.1.call-done), kind=kOutput, calls=%fused_computation.81 | convolution fusion | flops 1076887552 | bytes 6295552 | tf_op jit(solution)/shard_map/dot_general | solution.py:17
  151.0 5.4 %multiply_reduce_fusion = (f32[1024]{0:T(1024)S(1)}, f32[512]{0:T(512)S(1)}, f32[]{:T(128)}, f32[512]{0:T(512)S(1)}, f32[1024]{0:T(1024)S(1)}, /*index=5*/f32[512,1024]{1,0:T(8,128)S(1)}, bf16[512,1024]{1,0:T(8,128)(2,1)}) fusion(f32[512]{0:T(512)S(1)} %add_rsqrt_fusion, f32[512,1024]{1,0:T(8,128)S(1)} %get-tuple-element.268, ...), kind=kLoop, calls=%fused_computation.59 | loop fusion | flops 11006975 | bytes 7365132 | tf_op jit(solution)/shard_map/reduce_sum | solution.py:368
  159.0 7.3 %convolution_convert_fusion.1 = bf16[1024,4096]{1,0:T(8,128)(2,1)} fusion(bf16[512,1024]{1,0:T(8,128)(2,1)S(1)} %fusion.106, bf16[512,1024]{1,0:T(8,128)(2,1)S(1)} %get-tuple-element.259, bf16[512,1024]{1,0:T(8,128)(2,1)S(1)} %get-tuple-element.261, bf16[512,1024]{1,0:T(8,128)(2,1)S(1)} %copy-done.65, bf16[512,1024]{1,0:T(8,128)(2,1)S(1)} %copy-done.60), kind=kOutput, calls=%fused_computation.1 | convolution fusion | flops 4315938816 | bytes 13631488 | tf_op jit(solution)/shard_map/dot_general | solution.py:27
  170.7 4.0 multiply_convert_fusion
  174.8 4.2 multiply_convert_fusion.1
  204.2 7.0 %convolution_convert_fusion = bf16[1024,4096]{1,0:T(8,128)(2,1)S(1)} fusion(bf16[512,1024]{1,0:T(8,128)(2,1)} %copy-done.29, bf16[512,1024]{1,0:T(8,128)(2,1)} %copy-done.30, bf16[512,1024]{1,0:T(8,128)(2,1)} %copy-done.31, bf16[512,1024]{1,0:T(8,128)(2,1)} %copy-done.32, bf16[512,1024]{1,0:T(8,128)(2,1)S(1)} %multiply_convert_fusion.3), kind=kOutput, calls=%fused_computation | convolution fusion | flops 4315938816 | bytes 13631488 | tf_op jit(solution)/shard_map/dot_general | solution.py:27
  223.5 4.6 %all-to-all-start.2 = ((bf16[4,512,256]{2,1,0:T(8,128)(2,1)}), bf16[4,512,256]{2,1,0:T(8,128)(2,1)}, u32[]{:S(2)}, u32[]{:S(2)}) async-start(bf16[4,512,256]{2,1,0:T(8,128)(2,1)} %pad_maximum_fusion.5), calls=%async_computation.2 | async-start | bytes 2097152 | tf_op jit(solution)/shard_map/all_to_all | solution.py:306
  240.8 4.5 %reduce-scatter.3.cloned.1.call-done = bf16[128,4096]{1,0:T(8,128)(2,1)} async-done(((bf16[1024,4096]{1,0:T(8,128)(2,1)}), bf16[128,4096]{1,0:T(8,128)(2,1)}) %reduce-scatter.3.cloned.1.call-update) | async-done | bytes 1048592 | tf_op jit(solution)/shard_map/reduce_scatter | solution.py:365
  247.7 6.4 %all-to-all-done.2 = bf16[4,512,256]{2,1,0:T(8,128)(2,1)} async-done(((bf16[4,512,256]{2,1,0:T(8,128)(2,1)}), bf16[4,512,256]{2,1,0:T(8,128)(2,1)}, u32[]{:S(2)}, u32[]{:S(2)}) %all-to-all-start.2) | async-done | bytes 1048608 | tf_op jit(solution)/shard_map/all_to_all | solution.py:306
  259.6 28.8 %attend_backward.2 = bf16[2048,384]{1,0:T(8,128)(2,1)} custom-call(s32[1]{0:T(128)} %copy.70.length_ref, bf16[4,2048,128]{2,1,0:T(8,128)(2,1)} %get-tuple-element.89.extended_ref, bf16[2048,768]{1,0:T(8,128)(2,1)} %fusion.16.q_ref.k_ref.v_ref, bf16[2048,768]{1,0:T(8,128)(2,1)} %fusion.16.q_ref.k_ref.v_ref, bf16[2048,256]{1,0:T(8,128)(2,1)} %get-tuple-element.90.context_ref, ...), custom_call_target="tpu_custom_call" | custom-call | flops 21474836480 | bytes 5242880 | tf_op jit(solution)/shard_map/attend_backward/pallas_call | solution.py:208
  290.5 4.5 %all-to-all-start.4 = ((bf16[4,512,384]{2,1,0:T(8,128)(2,1)}), bf16[4,512,384]{2,1,0:T(8,128)(2,1)}, u32[]{:S(2)}, u32[]{:S(2)}) async-start(bf16[4,512,384]{2,1,0:T(8,128)(2,1)} %bitcast.241), calls=%async_computation.5 | async-start | bytes 3145728 | tf_op jit(solution)/shard_map/all_to_all | solution.py:306
  311.7 28.8 %attend_backward.3 = bf16[2048,384]{1,0:T(8,128)(2,1)} custom-call(s32[1]{0:T(128)} %copy.70.length_ref, bf16[4,2048,128]{2,1,0:T(8,128)(2,1)} %get-tuple-element.89.extended_ref, bf16[2048,768]{1,0:T(8,128)(2,1)} %fusion.16.q_ref.k_ref.v_ref, bf16[2048,768]{1,0:T(8,128)(2,1)} %fusion.16.q_ref.k_ref.v_ref, bf16[2048,256]{1,0:T(8,128)(2,1)} %get-tuple-element.90.context_ref, ...), custom_call_target="tpu_custom_call" | custom-call | flops 21474836480 | bytes 5242880 | tf_op jit(solution)/shard_map/attend_backward/pallas_call | solution.py:208
  340.5 5.5 %collective-permute-done.17 = f32[12,1024]{1,0:T(8,128)} collective-permute-done((f32[12,1024]{1,0:T(8,128)}, f32[12,1024]{1,0:T(8,128)}, u32[]{:S(2)}, u32[]{:S(2)}) %collective-permute-start.17) | collective-permute-done | bytes 49184 | tf_op jit(solution)/shard_map/ppermute | solution.py:243
  346.0 5.6 %collective-permute-done.15 = bf16[128,1024]{1,0:T(8,128)(2,1)} collective-permute-done((bf16[128,1024]{1,0:T(8,128)(2,1)S(1)}, bf16[128,1024]{1,0:T(8,128)(2,1)}, u32[]{:S(2)}, u32[]{:S(2)}) %collective-permute-start.15) | collective-permute-done | bytes 262176 | tf_op jit(solution)/shard_map/ppermute | solution.py:243
  351.7 6.4 %all-to-all-start.5 = ((bf16[4,512,384]{2,1,0:T(8,128)(2,1)}), bf16[4,512,384]{2,1,0:T(8,128)(2,1)}, u32[]{:S(2)}, u32[]{:S(2)}) async-start(bf16[4,512,384]{2,1,0:T(8,128)(2,1)} %bitcast.240), calls=%async_computation.7 | async-start | bytes 3145728 | tf_op jit(solution)/shard_map/all_to_all | solution.py:306
  359.6 4.1 convolution_convert_fusion.4
  394.4 5.0 %all-to-all-start.6 = ((bf16[4,136,256]{2,1,0:T(8,128)(2,1)}), bf16[4,136,256]{2,1,0:T(8,128)(2,1)S(1)}, u32[]{:S(2)}, u32[]{:S(2)}) async-start(bf16[4,136,256]{2,1,0:T(8,128)(2,1)} %pad_maximum_fusion.13), calls=%async_computation.8 | async-start | bytes 557056 | tf_op jit(solution)/shard_map/all_to_all | solution.py:306
  (377 shorter events, 185.0 us)
Async XLA Ops:
  9.6 20.7 %all-to-all-start = ((bf16[4,136,256]{2,1,0:T(8,128)(2,1)}), bf16[4,136,256]{2,1,0:T(8,128)(2,1)S(1)}, u32[]{:S(2)}, u32[]{:S(2)}) async-start(bf16[4,136,256]{2,1,0:T(8,128)(2,1)} %broadcast_in_dim.31), calls=%async_computation | async-start | bytes 557056 | tf_op jit(solution)/shard_map/all_to_all | solution.py:306
  16.0 97.3 %all-gather.4.cloned.1.call-start = ((), (), s32[]{:S(2)}) async-start(), calls=%async_computation.9 | async-start | bytes 6782976 | tf_op jit(solution)/shard_map/all_gather | solution.py:390
  35.5 102.5 %all-gather.6.cloned.1.call-start = ((), (), s32[]{:S(2)}) async-start(), calls=%async_computation.10 | async-start | bytes 9437184 | tf_op jit(solution)/shard_map/all_gather | solution.py:303
  35.5 36.3 %collective-permute-start.1 = (bf16[128,2048]{1,0:T(8,128)(2,1)S(1)}, bf16[128,2048]{1,0:T(8,128)(2,1)S(1)}, u32[]{:S(2)}, u32[]{:S(2)}) collective-permute-start(bf16[128,2048]{1,0:T(8,128)(2,1)S(1)} %fusion.81), channel_id=1, source_target_pairs={{0,2},{1,3},{2,0},{3,1},{4,6},{5,7},{6,4},{7,5},{8,10},{9,11},{10,... | collective-permute-start | bytes 1572872 | tf_op jit(solution)/shard_map/ppermute | solution.py:243
  37.6 34.2 %collective-permute-start.2 = (bf16[128,2048]{1,0:T(8,128)(2,1)S(1)}, bf16[128,2048]{1,0:T(8,128)(2,1)S(1)}, u32[]{:S(2)}, u32[]{:S(2)}) collective-permute-start(bf16[128,2048]{1,0:T(8,128)(2,1)S(1)} %fusion.81), channel_id=1, source_target_pairs={{0,3},{1,2},{2,1},{3,0},{4,7},{5,6},{6,5},{7,4},{8,11},{9,10},{10,... | collective-permute-start | bytes 1572872 | tf_op jit(solution)/shard_map/ppermute | solution.py:243
  73.0 40.1 %all-to-all-start.1 = ((bf16[4,512,256]{2,1,0:T(8,128)(2,1)}), bf16[4,512,256]{2,1,0:T(8,128)(2,1)S(1)}, u32[]{:S(2)}, u32[]{:S(2)}) async-start(bf16[4,512,256]{2,1,0:T(8,128)(2,1)} %bitcast.1), calls=%async_computation.1 | async-start | bytes 2097152 | tf_op jit(solution)/shard_map/all_to_all | solution.py:306
  87.3 158.0 %reduce-scatter.3.cloned.1.call-start = ((), (), s32[]{:S(2)}) async-start(), calls=%async_computation.11 | async-start | bytes 9437184 | tf_op jit(solution)/shard_map/reduce_scatter | solution.py:365
  166.3 35.7 %collective-permute-start.5 = (bf16[128,768]{1,0:T(8,128)(2,1)}, bf16[128,768]{1,0:T(8,128)(2,1)}, u32[]{:S(2)}, u32[]{:S(2)}) collective-permute-start(bf16[128,768]{1,0:T(8,128)(2,1)} %constant_dynamic-slice_fusion.16), channel_id=1, source_target_pairs={{0,3},{1,2},{2,1},{3,0},{4,7},{5,6},{6,5},{7,4},{8,11},{9,10},{10,... | collective-permute-start | bytes 589832 | tf_op jit(solution)/shard_map/ppermute | solution.py:243
  169.6 32.4 %collective-permute-start.4 = (bf16[128,768]{1,0:T(8,128)(2,1)}, bf16[128,768]{1,0:T(8,128)(2,1)}, u32[]{:S(2)}, u32[]{:S(2)}) collective-permute-start(bf16[128,768]{1,0:T(8,128)(2,1)} %constant_dynamic-slice_fusion.16), channel_id=1, source_target_pairs={{0,2},{1,3},{2,0},{3,1},{4,6},{5,7},{6,4},{7,5},{8,10},{9,11},{10,... | collective-permute-start | bytes 589832 | tf_op jit(solution)/shard_map/ppermute | solution.py:243
  169.6 32.4 %collective-permute-start.3 = (bf16[128,768]{1,0:T(8,128)(2,1)}, bf16[128,768]{1,0:T(8,128)(2,1)}, u32[]{:S(2)}, u32[]{:S(2)}) collective-permute-start(bf16[128,768]{1,0:T(8,128)(2,1)} %constant_dynamic-slice_fusion.16), channel_id=1, source_target_pairs={{0,1},{1,0},{2,3},{3,2},{4,5},{5,4},{6,7},{7,6},{8,9},{9,8},{10,11... | collective-permute-start | bytes 589832 | tf_op jit(solution)/shard_map/ppermute | solution.py:243
  223.5 30.6 %all-to-all-start.2 = ((bf16[4,512,256]{2,1,0:T(8,128)(2,1)}), bf16[4,512,256]{2,1,0:T(8,128)(2,1)}, u32[]{:S(2)}, u32[]{:S(2)}) async-start(bf16[4,512,256]{2,1,0:T(8,128)(2,1)} %pad_maximum_fusion.5), calls=%async_computation.2 | async-start | bytes 2097152 | tf_op jit(solution)/shard_map/all_to_all | solution.py:306
  235.1 53.4 %collective-permute-start.9 = (bf16[128,4096]{1,0:T(8,128)(2,1)}, bf16[128,4096]{1,0:T(8,128)(2,1)S(1)}, u32[]{:S(2)}, u32[]{:S(2)}) collective-permute-start(bf16[128,4096]{1,0:T(8,128)(2,1)} %pad_maximum_fusion.8), channel_id=1, source_target_pairs={{0,8},{4,12},{8,0},{12,4},{16,24},{20,28},{24,16},{28,20},{1,9},{5... | collective-permute-start | bytes 3145736 | tf_op jit(solution)/shard_map/ppermute | solution.py:243
  237.6 50.8 %collective-permute-start.10 = (bf16[128,4096]{1,0:T(8,128)(2,1)}, bf16[128,4096]{1,0:T(8,128)(2,1)}, u32[]{:S(2)}, u32[]{:S(2)}) collective-permute-start(bf16[128,4096]{1,0:T(8,128)(2,1)} %pad_maximum_fusion.9), channel_id=1, source_target_pairs={{0,16},{4,20},{8,24},{12,28},{16,0},{20,4},{24,8},{28,12},{1,17},{... | collective-permute-start | bytes 3145736 | tf_op jit(solution)/shard_map/ppermute | solution.py:243
  239.8 48.7 %collective-permute-start.11 = (bf16[128,4096]{1,0:T(8,128)(2,1)}, bf16[128,4096]{1,0:T(8,128)(2,1)}, u32[]{:S(2)}, u32[]{:S(2)}) collective-permute-start(bf16[128,4096]{1,0:T(8,128)(2,1)} %pad_maximum_fusion.10), channel_id=1, source_target_pairs={{0,24},{4,28},{8,16},{12,20},{16,8},{20,12},{24,0},{28,4},{1,25},{... | collective-permute-start | bytes 3145736 | tf_op jit(solution)/shard_map/ppermute | solution.py:243
  254.1 34.4 %all-to-all-start.3 = ((bf16[4,128,1024]{2,1,0:T(8,128)(2,1)}), bf16[4,128,1024]{2,1,0:T(8,128)(2,1)S(1)}, u32[]{:S(2)}, u32[]{:S(2)}) async-start(bf16[4,128,1024]{2,1,0:T(8,128)(2,1)} %pad_maximum_fusion.6), calls=%async_computation.4 | async-start | bytes 2097152 | tf_op jit(solution)/shard_map/all_to_all | solution.py:306
  257.6 94.0 %reduce-scatter.5.cloned.1.call-start = ((), (), s32[]{:S(2)}) async-start(), calls=%async_computation.12 | async-start | bytes 2359296 | tf_op jit(solution)/shard_map/reduce_scatter | solution.py:365
  257.7 30.8 %collective-permute-start.12 = (f32[12,1024]{1,0:T(8,128)S(1)}, f32[12,1024]{1,0:T(8,128)S(1)}, u32[]{:S(2)}, u32[]{:S(2)}) collective-permute-start(f32[12,1024]{1,0:T(8,128)S(1)} %add.423), channel_id=1, source_target_pairs={{0,1},{1,0},{2,3},{3,2},{4,5},{5,4},{6,7},{7,6},{8,9},{9,8},{10,11... | collective-permute-start | bytes 147464 | tf_op jit(solution)/shard_map/ppermute | solution.py:243
  290.5 61.2 %all-to-all-start.4 = ((bf16[4,512,384]{2,1,0:T(8,128)(2,1)}), bf16[4,512,384]{2,1,0:T(8,128)(2,1)}, u32[]{:S(2)}, u32[]{:S(2)}) async-start(bf16[4,512,384]{2,1,0:T(8,128)(2,1)} %bitcast.241), calls=%async_computation.5 | async-start | bytes 3145728 | tf_op jit(solution)/shard_map/all_to_all | solution.py:306
  295.0 113.8 %all-gather.8.cloned.1.call-start = ((), (), s32[]{:S(2)}) async-start(), calls=%async_computation.13 | async-start | bytes 5308416 | tf_op jit(solution)/shard_map/all_gather | solution.py:303
  295.3 50.8 %collective-permute-start.17 = (f32[12,1024]{1,0:T(8,128)}, f32[12,1024]{1,0:T(8,128)}, u32[]{:S(2)}, u32[]{:S(2)}) collective-permute-start(f32[12,1024]{1,0:T(8,128)} %add.436), channel_id=1, source_target_pairs={{0,2},{1,3},{2,0},{3,1},{4,6},{5,7},{6,4},{7,5},{8,10},{9,11},{10,... | collective-permute-start | bytes 147464 | tf_op jit(solution)/shard_map/ppermute | solution.py:243
  307.3 38.8 %collective-permute-start.14 = (bf16[128,1024]{1,0:T(8,128)(2,1)S(1)}, bf16[128,1024]{1,0:T(8,128)(2,1)}, u32[]{:S(2)}, u32[]{:S(2)}) collective-permute-start(bf16[128,1024]{1,0:T(8,128)(2,1)S(1)} %get-tuple-element.104), channel_id=1, source_target_pairs={{0,1},{1,0},{2,3},{3,2},{4,5},{5,4},{6,7},{7,6},{8,9},{9,8},{10,11... | collective-permute-start | bytes 786440 | tf_op jit(solution)/shard_map/ppermute | solution.py:243
  308.8 42.8 %collective-permute-start.15 = (bf16[128,1024]{1,0:T(8,128)(2,1)S(1)}, bf16[128,1024]{1,0:T(8,128)(2,1)}, u32[]{:S(2)}, u32[]{:S(2)}) collective-permute-start(bf16[128,1024]{1,0:T(8,128)(2,1)S(1)} %get-tuple-element.105), channel_id=1, source_target_pairs={{0,2},{1,3},{2,0},{3,1},{4,6},{5,7},{6,4},{7,5},{8,10},{9,11},{10,... | collective-permute-start | bytes 786440 | tf_op jit(solution)/shard_map/ppermute | solution.py:243
  309.5 42.2 %collective-permute-start.16 = (bf16[128,1024]{1,0:T(8,128)(2,1)S(1)}, bf16[128,1024]{1,0:T(8,128)(2,1)}, u32[]{:S(2)}, u32[]{:S(2)}) collective-permute-start(bf16[128,1024]{1,0:T(8,128)(2,1)S(1)} %get-tuple-element.106), channel_id=1, source_target_pairs={{0,3},{1,2},{2,1},{3,0},{4,7},{5,6},{6,5},{7,4},{8,11},{9,10},{10,... | collective-permute-start | bytes 786440 | tf_op jit(solution)/shard_map/ppermute | solution.py:243
  351.7 42.8 %all-to-all-start.5 = ((bf16[4,512,384]{2,1,0:T(8,128)(2,1)}), bf16[4,512,384]{2,1,0:T(8,128)(2,1)}, u32[]{:S(2)}, u32[]{:S(2)}) async-start(bf16[4,512,384]{2,1,0:T(8,128)(2,1)} %bitcast.240), calls=%async_computation.7 | async-start | bytes 3145728 | tf_op jit(solution)/shard_map/all_to_all | solution.py:306
  (85 other events, 487.5 us)
Sparse Core Ops, SparseCore 0:
  35.6 43.9 all-gather.3
  82.0 55.8 all-gather.5
  170.8 74.4 reduce-scatter.2
  290.0 40.1 reduce-scatter.4
  331.9 39.9 all-gather.7

commit v2 on v1

--- a/solution.py
+++ b/solution.py
@@ -445,14 +445,16 @@
     first_grad = norm_back(normed_grad, normal_one, inverse_one, first_gain)
     attention_low = first_grad.astype(jnp.bfloat16)
     grad_all = matmul(attention_low, output_weight_all).astype(jnp.bfloat16)
-    grad_all, inner_lows, qkv_parts = tie(grad_all, inner_lows, qkv_parts)
+    grad_all, inner_lows, qkv_parts, attention_late = tie(
+        grad_all, inner_lows, qkv_parts, attention_low
+    )
     context_grad = trade(column_blocks(grad_all)).reshape(seq_len, heads_width)
     inner_whole = over_rows(normed_low, jnp.concatenate(inner_lows, axis=1)).astype(jnp.bfloat16)
     inner_kept = [
         with_other_core(half_rows(half, 0), half_rows(half, 1))
         for half in jnp.split(inner_whole, 2, axis=1)
     ]
-    output_whole = over_rows(attention_low, context_all).astype(jnp.bfloat16)
+    output_whole = over_rows(attention_late, context_all).astype(jnp.bfloat16)
     inner_chips = to_chips(inner_kept)
     vectors = [
         ordered(jnp.concatenate([column_sums(low) for low in inner_lows])),

time: 435 us -> 435 us (level)
    unnamed x166 -> x214, local copies, waits for them, and re-layouts: 20.8 us -> 19.6 us
where the time goes in v2:
time: 435 us; the launch traced here: 428 us
  Pallas kernels  88.8 us (20%)
  matrix products  82.3 us (19%)
  starting transfers between devices  73.2 us (17%)
  waiting for transfers between devices  71.3 us (16%)
  other arithmetic  47.4 us (11%)
  local copies, waits for them, and re-layouts  45 us (10%)
  between operations  19.9 us (5%)
    pallas_call x2, Pallas kernels, attend_backward(): pl.pallas_call(backward_kernel, grid_spec=pltpu.PrefetchScalarGridSpec(nu...  57.6 us
    all_to_all x7, starting transfers between devices, trade(): return lax.all_to_all(blocks, 'tensor', 0, 0)  43.9 us
    dot_general x14, matrix products, matmul(): return jnp.dot(former, latter, preferred_element_type=jnp.float32)  42.3 us
    pallas_call x1, Pallas kernels, attend_forward(): pl.pallas_call(forward_kernel, grid_spec=pltpu.PrefetchScalarGridSpec(num...  31.1 us
    ppermute x25, waiting for transfers between devices, flip(): lax.ppermute(array_in, axis_name, [(i, i ^ bits) for i in range(size)])  29.4 us
    ppermute x25, starting transfers between devices, flip(): lax.ppermute(array_in, axis_name, [(i, i ^ bits) for i in range(size)])  28.9 us
    all_to_all x7, waiting for transfers between devices, trade(): return lax.all_to_all(blocks, 'tensor', 0, 0)  26.5 us
    dot_general x11, matrix products, times_rows(): lax.dot_general(former, latter, (((1,), (1,)), ((), ())), preferred_eleme...  22.7 us
  transfers between devices with their start and end apart: 37, of which 15 were waited for; matrix products, arithmetic and copies ran while one was open for 29% of the time, Pallas kernels for 21%

profile of v2, /device:TPU:0, one launch (start us, length us, event | category | flops | bytes accessed | tf_op | source)
XLA Modules:
  0.0 427.8 jit_solution(4152281101405727077)
XLA Ops:
  9.6 6.3 %all-to-all-start = ((bf16[4,136,256]{2,1,0:T(8,128)(2,1)}), bf16[4,136,256]{2,1,0:T(8,128)(2,1)S(1)}, u32[]{:S(2)}, u32[]{:S(2)}) async-start(bf16[4,136,256]{2,1,0:T(8,128)(2,1)} %broadcast_in_dim.31), calls=%async_computation | async-start | bytes 557056 | tf_op jit(solution)/shard_map/all_to_all | solution.py:306
  24.9 4.7 %fusion.16.q_ref.k_ref.v_ref = bf16[2048,768]{1,0:T(8,128)(2,1)} fusion(f32[768]{0:T(1024)S(1)} %convert_element_type.339, bf16[2048,1024]{1,0:T(8,128)(2,1)S(1)} %copy-done.12, bf16[1024,768]{1,0:T(8,128)(2,1)S(1)} %get-tuple-element.199), kind=kOutput, calls=%fused_computation.27 | convolution fusion | flops 3224371200 | bytes 8915968 | tf_op jit(solution)/shard_map/dot_general | solution.py:17
  30.3 4.1 collective-permute-done
  37.8 31.1 %attend_forward.1 = (bf16[2048,256]{1,0:T(8,128)(2,1)}, bf16[4,2048,128]{2,1,0:T(8,128)(2,1)}) custom-call(s32[1]{0:T(128)} %copy.70.length_ref, bf16[2048,768]{1,0:T(8,128)(2,1)} %fusion.16.q_ref.k_ref.v_ref, bf16[2048,768]{1,0:T(8,128)(2,1)} %fusion.16.q_ref.k_ref.v_ref, bf16[2048,768]{1,0:T(8,128)(2,1)} %fusion.16.q_ref.k_ref.v_ref), custom_call_target="tpu_custom_call" | custom-call | flops 17179869184 | bytes 6291456 | tf_op jit(solution)/shard_map/attend_forward/pallas_call | solution.py:115
  73.1 14.3 %all-to-all-start.1 = ((bf16[4,512,256]{2,1,0:T(8,128)(2,1)}), bf16[4,512,256]{2,1,0:T(8,128)(2,1)S(1)}, u32[]{:S(2)}, u32[]{:S(2)}) async-start(bf16[4,512,256]{2,1,0:T(8,128)(2,1)} %bitcast.1), calls=%async_computation.1 | async-start | bytes 2097152 | tf_op jit(solution)/shard_map/all_to_all | solution.py:306
  94.9 18.3 %all-to-all-done.1 = bf16[4,512,256]{2,1,0:T(8,128)(2,1)S(1)} async-done(((bf16[4,512,256]{2,1,0:T(8,128)(2,1)}), bf16[4,512,256]{2,1,0:T(8,128)(2,1)S(1)}, u32[]{:S(2)}, u32[]{:S(2)}) %all-to-all-start.1) | async-done | bytes 1048608 | tf_op jit(solution)/shard_map/all_to_all | solution.py:306
  130.3 7.7 %all-gather.6.cloned.1.call-done = bf16[4,1024,1024]{2,1,0:T(8,128)(2,1)} async-done(((bf16[4,128,1024]{2,1,0:T(8,128)(2,1)}), bf16[4,1024,1024]{2,1,0:T(8,128)(2,1)}) %all-gather.6.cloned.1.call-update) | async-done | bytes 8388624 | tf_op jit(solution)/shard_map/all_gather | solution.py:303
  138.0 4.5 %multiply_convert_fusion.4 = (bf16[512,1024]{1,0:T(8,128)(2,1)S(1)}, f32[512,1024]{1,0:T(8,128)}) fusion(f32[1024]{0:T(1024)S(1)} %bitcast.281, bf16[512,1024]{1,0:T(8,128)(2,1)S(1)} %fusion.37, bf16[4,1024,1024]{2,1,0:T(8,128)(2,1)} %all-gather.6.cloned.1.call-done), kind=kOutput, calls=%fused_computation.81 | convolution fusion | flops 1076887552 | bytes 6295552 | tf_op jit(solution)/shard_map/dot_general | solution.py:17
  151.1 5.5 %multiply_reduce_fusion = (f32[1024]{0:T(1024)}, f32[512]{0:T(512)S(1)}, f32[]{:T(128)}, f32[512]{0:T(512)S(1)}, f32[1024]{0:T(1024)}, /*index=5*/f32[512,1024]{1,0:T(8,128)S(1)}, bf16[512,1024]{1,0:T(8,128)(2,1)}) fusion(f32[512]{0:T(512)S(1)} %add_rsqrt_fusion, f32[512,1024]{1,0:T(8,128)S(1)} %get-tuple-element.271, f32[512]{0:T(512)S(1)} %broadcast_multiply_fusion.4, ...), kind=kLoop, calls=%fused_computation.59 | loop fusion | flops 11006975 | bytes 7365132 | tf_op jit(solution)/shard_map/reduce_sum | solution.py:368
  159.2 7.3 %convolution_convert_fusion.1 = bf16[1024,4096]{1,0:T(8,128)(2,1)} fusion(bf16[512,1024]{1,0:T(8,128)(2,1)S(1)} %fusion.104, bf16[512,1024]{1,0:T(8,128)(2,1)S(1)} %get-tuple-element.262, bf16[512,1024]{1,0:T(8,128)(2,1)S(1)} %get-tuple-element.264, bf16[512,1024]{1,0:T(8,128)(2,1)S(1)} %copy-done.89, bf16[512,1024]{1,0:T(8,128)(2,1)S(1)} %copy-done.84), kind=kOutput, calls=%fused_computation.1 | convolution fusion | flops 4315938816 | bytes 13631488 | tf_op jit(solution)/shard_map/dot_general | solution.py:27
  171.0 4.0 multiply_convert_fusion
  175.0 4.3 %multiply_convert_fusion.1 = bf16[512,1024]{1,0:T(8,128)(2,1)S(1)} fusion(bf16[512,1024]{1,0:T(8,128)(2,1)S(1)} %fusion.104, bf16[4,1024,1024]{2,1,0:T(8,128)(2,1)} %all-gather.6.cloned.1.call-done, f32[512,1024]{1,0:T(8,128)S(1)} %copy-done.87, f32[1024]{0:T(1024)S(1)} %bitcast.280), kind=kOutput, calls=%fused_computation.71 | convolution fusion | flops 1080557568 | bytes 6295552 | tf_op jit(solution)/shard_map/dot_general | solution.py:17
  200.6 6.1 %convolution_convert_fusion = bf16[1024,4096]{1,0:T(8,128)(2,1)S(1)} fusion(bf16[512,1024]{1,0:T(8,128)(2,1)S(1)} %copy-done.30, bf16[512,1024]{1,0:T(8,128)(2,1)S(1)} %copy-done.32, bf16[512,1024]{1,0:T(8,128)(2,1)} %copy-done.34, bf16[512,1024]{1,0:T(8,128)(2,1)} %copy-done.36, bf16[512,1024]{1,0:T(8,128)(2,1)S(1)} %multiply_convert_fusion.3), kind=kOutput, calls=%fused_computation | convolution fusion | flops 4315938816 | bytes 13631488 | tf_op jit(solution)/shard_map/dot_general | solution.py:27
  221.6 4.5 %all-to-all-start.2 = ((bf16[4,512,256]{2,1,0:T(8,128)(2,1)}), bf16[4,512,256]{2,1,0:T(8,128)(2,1)}, u32[]{:S(2)}, u32[]{:S(2)}) async-start(bf16[4,512,256]{2,1,0:T(8,128)(2,1)} %pad_maximum_fusion.5), calls=%async_computation.2 | async-start | bytes 2097152 | tf_op jit(solution)/shard_map/all_to_all | solution.py:306
  239.4 7.5 %reduce-scatter.3.cloned.1.call-done = bf16[128,4096]{1,0:T(8,128)(2,1)} async-done(((bf16[1024,4096]{1,0:T(8,128)(2,1)}), bf16[128,4096]{1,0:T(8,128)(2,1)}) %reduce-scatter.3.cloned.1.call-update) | async-done | bytes 1048592 | tf_op jit(solution)/shard_map/reduce_scatter | solution.py:365
  258.1 28.9 %attend_backward.2 = bf16[2048,384]{1,0:T(8,128)(2,1)} custom-call(s32[1]{0:T(128)} %copy.70.length_ref, bf16[4,2048,128]{2,1,0:T(8,128)(2,1)} %get-tuple-element.91.extended_ref, bf16[2048,768]{1,0:T(8,128)(2,1)} %fusion.16.q_ref.k_ref.v_ref, bf16[2048,768]{1,0:T(8,128)(2,1)} %fusion.16.q_ref.k_ref.v_ref, bf16[2048,256]{1,0:T(8,128)(2,1)} %get-tuple-element.92.context_ref, ...), custom_call_target="tpu_custom_call" | custom-call | flops 21474836480 | bytes 5242880 | tf_op jit(solution)/shard_map/attend_backward/pallas_call | solution.py:208
  289.0 4.5 %all-to-all-start.4 = ((bf16[4,512,384]{2,1,0:T(8,128)(2,1)}), bf16[4,512,384]{2,1,0:T(8,128)(2,1)}, u32[]{:S(2)}, u32[]{:S(2)}) async-start(bf16[4,512,384]{2,1,0:T(8,128)(2,1)} %bitcast.243), calls=%async_computation.5 | async-start | bytes 3145728 | tf_op jit(solution)/shard_map/all_to_all | solution.py:306
  310.2 28.8 %attend_backward.3 = bf16[2048,384]{1,0:T(8,128)(2,1)} custom-call(s32[1]{0:T(128)} %copy.70.length_ref, bf16[4,2048,128]{2,1,0:T(8,128)(2,1)} %get-tuple-element.91.extended_ref, bf16[2048,768]{1,0:T(8,128)(2,1)} %fusion.16.q_ref.k_ref.v_ref, bf16[2048,768]{1,0:T(8,128)(2,1)} %fusion.16.q_ref.k_ref.v_ref, bf16[2048,256]{1,0:T(8,128)(2,1)} %get-tuple-element.92.context_ref, ...), custom_call_target="tpu_custom_call" | custom-call | flops 21474836480 | bytes 5242880 | tf_op jit(solution)/shard_map/attend_backward/pallas_call | solution.py:208
  339.0 6.6 %collective-permute-done.17 = f32[12,1024]{1,0:T(8,128)} collective-permute-done((f32[12,1024]{1,0:T(8,128)}, f32[12,1024]{1,0:T(8,128)}, u32[]{:S(2)}, u32[]{:S(2)}) %collective-permute-start.17) | collective-permute-done | bytes 49184 | tf_op jit(solution)/shard_map/ppermute | solution.py:243
  345.6 5.6 %collective-permute-done.15 = bf16[128,1024]{1,0:T(8,128)(2,1)} collective-permute-done((bf16[128,1024]{1,0:T(8,128)(2,1)S(1)}, bf16[128,1024]{1,0:T(8,128)(2,1)}, u32[]{:S(2)}, u32[]{:S(2)}) %collective-permute-start.15) | collective-permute-done | bytes 262176 | tf_op jit(solution)/shard_map/ppermute | solution.py:243
  351.2 6.4 %all-to-all-start.5 = ((bf16[4,512,384]{2,1,0:T(8,128)(2,1)}), bf16[4,512,384]{2,1,0:T(8,128)(2,1)}, u32[]{:S(2)}, u32[]{:S(2)}) async-start(bf16[4,512,384]{2,1,0:T(8,128)(2,1)} %bitcast.242), calls=%async_computation.7 | async-start | bytes 3145728 | tf_op jit(solution)/shard_map/all_to_all | solution.py:306
  359.1 4.1 convolution_convert_fusion.4
  394.3 4.3 %all-to-all-start.6 = ((bf16[4,136,256]{2,1,0:T(8,128)(2,1)}), bf16[4,136,256]{2,1,0:T(8,128)(2,1)S(1)}, u32[]{:S(2)}, u32[]{:S(2)}) async-start(bf16[4,136,256]{2,1,0:T(8,128)(2,1)} %pad_maximum_fusion.13), calls=%async_computation.8 | async-start | bytes 557056 | tf_op jit(solution)/shard_map/all_to_all | solution.py:306
  403.2 4.0 all-to-all-done.6
  (425 shorter events, 184.6 us)
Async XLA Ops:
  9.6 20.7 %all-to-all-start = ((bf16[4,136,256]{2,1,0:T(8,128)(2,1)}), bf16[4,136,256]{2,1,0:T(8,128)(2,1)S(1)}, u32[]{:S(2)}, u32[]{:S(2)}) async-start(bf16[4,136,256]{2,1,0:T(8,128)(2,1)} %broadcast_in_dim.31), calls=%async_computation | async-start | bytes 557056 | tf_op jit(solution)/shard_map/all_to_all | solution.py:306
  16.0 97.3 %all-gather.4.cloned.1.call-start = ((), (), s32[]{:S(2)}) async-start(), calls=%async_computation.9 | async-start | bytes 6782976 | tf_op jit(solution)/shard_map/all_gather | solution.py:390
  35.5 102.5 %all-gather.6.cloned.1.call-start = ((), (), s32[]{:S(2)}) async-start(), calls=%async_computation.10 | async-start | bytes 9437184 | tf_op jit(solution)/shard_map/all_gather | solution.py:303
  35.5 36.3 %collective-permute-start.1 = (bf16[128,2048]{1,0:T(8,128)(2,1)S(1)}, bf16[128,2048]{1,0:T(8,128)(2,1)S(1)}, u32[]{:S(2)}, u32[]{:S(2)}) collective-permute-start(bf16[128,2048]{1,0:T(8,128)(2,1)S(1)} %fusion.81), channel_id=1, source_target_pairs={{0,2},{1,3},{2,0},{3,1},{4,6},{5,7},{6,4},{7,5},{8,10},{9,11},{10,... | collective-permute-start | bytes 1572872 | tf_op jit(solution)/shard_map/ppermute | solution.py:243
  37.6 34.2 %collective-permute-start.2 = (bf16[128,2048]{1,0:T(8,128)(2,1)S(1)}, bf16[128,2048]{1,0:T(8,128)(2,1)S(1)}, u32[]{:S(2)}, u32[]{:S(2)}) collective-permute-start(bf16[128,2048]{1,0:T(8,128)(2,1)S(1)} %fusion.81), channel_id=1, source_target_pairs={{0,3},{1,2},{2,1},{3,0},{4,7},{5,6},{6,5},{7,4},{8,11},{9,10},{10,... | collective-permute-start | bytes 1572872 | tf_op jit(solution)/shard_map/ppermute | solution.py:243
  73.1 40.1 %all-to-all-start.1 = ((bf16[4,512,256]{2,1,0:T(8,128)(2,1)}), bf16[4,512,256]{2,1,0:T(8,128)(2,1)S(1)}, u32[]{:S(2)}, u32[]{:S(2)}) async-start(bf16[4,512,256]{2,1,0:T(8,128)(2,1)} %bitcast.1), calls=%async_computation.1 | async-start | bytes 2097152 | tf_op jit(solution)/shard_map/all_to_all | solution.py:306
  87.3 159.6 %reduce-scatter.3.cloned.1.call-start = ((), (), s32[]{:S(2)}) async-start(), calls=%async_computation.11 | async-start | bytes 9437184 | tf_op jit(solution)/shard_map/reduce_scatter | solution.py:365
  166.5 32.1 %collective-permute-start.5 = (bf16[128,768]{1,0:T(8,128)(2,1)}, bf16[128,768]{1,0:T(8,128)(2,1)S(1)}, u32[]{:S(2)}, u32[]{:S(2)}) collective-permute-start(bf16[128,768]{1,0:T(8,128)(2,1)} %constant_dynamic-slice_fusion.16), channel_id=1, source_target_pairs={{0,3},{1,2},{2,1},{3,0},{4,7},{5,6},{6,5},{7,4},{8,11},{9,10},{10,... | collective-permute-start | bytes 589832 | tf_op jit(solution)/shard_map/ppermute | solution.py:243
  169.9 28.8 %collective-permute-start.4 = (bf16[128,768]{1,0:T(8,128)(2,1)}, bf16[128,768]{1,0:T(8,128)(2,1)S(1)}, u32[]{:S(2)}, u32[]{:S(2)}) collective-permute-start(bf16[128,768]{1,0:T(8,128)(2,1)} %constant_dynamic-slice_fusion.16), channel_id=1, source_target_pairs={{0,2},{1,3},{2,0},{3,1},{4,6},{5,7},{6,4},{7,5},{8,10},{9,11},{10,... | collective-permute-start | bytes 589832 | tf_op jit(solution)/shard_map/ppermute | solution.py:243
  169.9 28.8 %collective-permute-start.3 = (bf16[128,768]{1,0:T(8,128)(2,1)}, bf16[128,768]{1,0:T(8,128)(2,1)}, u32[]{:S(2)}, u32[]{:S(2)}) collective-permute-start(bf16[128,768]{1,0:T(8,128)(2,1)} %constant_dynamic-slice_fusion.16), channel_id=1, source_target_pairs={{0,1},{1,0},{2,3},{3,2},{4,5},{5,4},{6,7},{7,6},{8,9},{9,8},{10,11... | collective-permute-start | bytes 589832 | tf_op jit(solution)/shard_map/ppermute | solution.py:243
  221.6 31.0 %all-to-all-start.2 = ((bf16[4,512,256]{2,1,0:T(8,128)(2,1)}), bf16[4,512,256]{2,1,0:T(8,128)(2,1)}, u32[]{:S(2)}, u32[]{:S(2)}) async-start(bf16[4,512,256]{2,1,0:T(8,128)(2,1)} %pad_maximum_fusion.5), calls=%async_computation.2 | async-start | bytes 2097152 | tf_op jit(solution)/shard_map/all_to_all | solution.py:306
  233.7 53.3 %collective-permute-start.9 = (bf16[128,4096]{1,0:T(8,128)(2,1)}, bf16[128,4096]{1,0:T(8,128)(2,1)S(1)}, u32[]{:S(2)}, u32[]{:S(2)}) collective-permute-start(bf16[128,4096]{1,0:T(8,128)(2,1)} %pad_maximum_fusion.8), channel_id=1, source_target_pairs={{0,8},{4,12},{8,0},{12,4},{16,24},{20,28},{24,16},{28,20},{1,9},{5... | collective-permute-start | bytes 3145736 | tf_op jit(solution)/shard_map/ppermute | solution.py:243
  235.9 51.1 %collective-permute-start.10 = (bf16[128,4096]{1,0:T(8,128)(2,1)}, bf16[128,4096]{1,0:T(8,128)(2,1)}, u32[]{:S(2)}, u32[]{:S(2)}) collective-permute-start(bf16[128,4096]{1,0:T(8,128)(2,1)} %pad_maximum_fusion.9), channel_id=1, source_target_pairs={{0,16},{4,20},{8,24},{12,28},{16,0},{20,4},{24,8},{28,12},{1,17},{... | collective-permute-start | bytes 3145736 | tf_op jit(solution)/shard_map/ppermute | solution.py:243
  237.4 49.6 %collective-permute-start.11 = (bf16[128,4096]{1,0:T(8,128)(2,1)}, bf16[128,4096]{1,0:T(8,128)(2,1)}, u32[]{:S(2)}, u32[]{:S(2)}) collective-permute-start(bf16[128,4096]{1,0:T(8,128)(2,1)} %pad_maximum_fusion.10), channel_id=1, source_target_pairs={{0,24},{4,28},{8,16},{12,20},{16,8},{20,12},{24,0},{28,4},{1,25},{... | collective-permute-start | bytes 3145736 | tf_op jit(solution)/shard_map/ppermute | solution.py:243
  252.6 34.4 %all-to-all-start.3 = ((bf16[4,128,1024]{2,1,0:T(8,128)(2,1)}), bf16[4,128,1024]{2,1,0:T(8,128)(2,1)S(1)}, u32[]{:S(2)}, u32[]{:S(2)}) async-start(bf16[4,128,1024]{2,1,0:T(8,128)(2,1)} %pad_maximum_fusion.6), calls=%async_computation.4 | async-start | bytes 2097152 | tf_op jit(solution)/shard_map/all_to_all | solution.py:306
  256.1 95.1 %reduce-scatter.5.cloned.1.call-start = ((), (), s32[]{:S(2)}) async-start(), calls=%async_computation.12 | async-start | bytes 2359296 | tf_op jit(solution)/shard_map/reduce_scatter | solution.py:365
  256.2 30.8 %collective-permute-start.12 = (f32[12,1024]{1,0:T(8,128)S(1)}, f32[12,1024]{1,0:T(8,128)S(1)}, u32[]{:S(2)}, u32[]{:S(2)}) collective-permute-start(f32[12,1024]{1,0:T(8,128)S(1)} %add.423), channel_id=1, source_target_pairs={{0,1},{1,0},{2,3},{3,2},{4,5},{5,4},{6,7},{7,6},{8,9},{9,8},{10,11... | collective-permute-start | bytes 147464 | tf_op jit(solution)/shard_map/ppermute | solution.py:243
  289.0 62.2 %all-to-all-start.4 = ((bf16[4,512,384]{2,1,0:T(8,128)(2,1)}), bf16[4,512,384]{2,1,0:T(8,128)(2,1)}, u32[]{:S(2)}, u32[]{:S(2)}) async-start(bf16[4,512,384]{2,1,0:T(8,128)(2,1)} %bitcast.243), calls=%async_computation.5 | async-start | bytes 3145728 | tf_op jit(solution)/shard_map/all_to_all | solution.py:306
  293.5 115.0 %all-gather.8.cloned.1.call-start = ((), (), s32[]{:S(2)}) async-start(), calls=%async_computation.13 | async-start | bytes 5308416 | tf_op jit(solution)/shard_map/all_gather | solution.py:303
  293.8 51.8 %collective-permute-start.17 = (f32[12,1024]{1,0:T(8,128)}, f32[12,1024]{1,0:T(8,128)}, u32[]{:S(2)}, u32[]{:S(2)}) collective-permute-start(f32[12,1024]{1,0:T(8,128)} %add.436), channel_id=1, source_target_pairs={{0,2},{1,3},{2,0},{3,1},{4,6},{5,7},{6,4},{7,5},{8,10},{9,11},{10,... | collective-permute-start | bytes 147464 | tf_op jit(solution)/shard_map/ppermute | solution.py:243
  305.8 39.8 %collective-permute-start.14 = (bf16[128,1024]{1,0:T(8,128)(2,1)S(1)}, bf16[128,1024]{1,0:T(8,128)(2,1)}, u32[]{:S(2)}, u32[]{:S(2)}) collective-permute-start(bf16[128,1024]{1,0:T(8,128)(2,1)S(1)} %get-tuple-element.106), channel_id=1, source_target_pairs={{0,1},{1,0},{2,3},{3,2},{4,5},{5,4},{6,7},{7,6},{8,9},{9,8},{10,11... | collective-permute-start | bytes 786440 | tf_op jit(solution)/shard_map/ppermute | solution.py:243
  307.3 43.9 %collective-permute-start.15 = (bf16[128,1024]{1,0:T(8,128)(2,1)S(1)}, bf16[128,1024]{1,0:T(8,128)(2,1)}, u32[]{:S(2)}, u32[]{:S(2)}) collective-permute-start(bf16[128,1024]{1,0:T(8,128)(2,1)S(1)} %get-tuple-element.107), channel_id=1, source_target_pairs={{0,2},{1,3},{2,0},{3,1},{4,6},{5,7},{6,4},{7,5},{8,10},{9,11},{10,... | collective-permute-start | bytes 786440 | tf_op jit(solution)/shard_map/ppermute | solution.py:243
  308.0 43.2 %collective-permute-start.16 = (bf16[128,1024]{1,0:T(8,128)(2,1)S(1)}, bf16[128,1024]{1,0:T(8,128)(2,1)}, u32[]{:S(2)}, u32[]{:S(2)}) collective-permute-start(bf16[128,1024]{1,0:T(8,128)(2,1)S(1)} %get-tuple-element.108), channel_id=1, source_target_pairs={{0,3},{1,2},{2,1},{3,0},{4,7},{5,6},{6,5},{7,4},{8,11},{9,10},{10,... | collective-permute-start | bytes 786440 | tf_op jit(solution)/shard_map/ppermute | solution.py:243
  351.2 43.1 %all-to-all-start.5 = ((bf16[4,512,384]{2,1,0:T(8,128)(2,1)}), bf16[4,512,384]{2,1,0:T(8,128)(2,1)}, u32[]{:S(2)}, u32[]{:S(2)}) async-start(bf16[4,512,384]{2,1,0:T(8,128)(2,1)} %bitcast.242), calls=%async_computation.7 | async-start | bytes 3145728 | tf_op jit(solution)/shard_map/all_to_all | solution.py:306
  (109 other events, 758.7 us)
Sparse Core Ops, SparseCore 0:
  35.6 43.9 all-gather.3
  82.1 55.8 all-gather.5
  171.1 75.8 reduce-scatter.2
  288.5 40.1 reduce-scatter.4
  330.4 38.7 all-gather.7
